TPU v7x, 32 devices: a whole 2x2x4 slice. The times are simulated.
32 devices in a mesh: cells: 2 (over x), fh: 16 (over z, y, core).
Axes of the slice: x: 2, y: 2, z: 4, core: 2. Of those that a mesh axis runs over, the one named last changes fastest.
Arguments:
- received_time_rows: bfloat16 [4096, 3, 2, 4096], P(('cells', 'fh')), parts along dimension 0, may hold values from -24 to 24
- pilots: int32 [128], P('cells'), parts along dimension 0, may hold values from 0 to 63, as said below
- active_users: int32 [128], P('cells'), parts along dimension 0, may hold values 0 or 1
- allocation: int32 [256, 64], P(('cells', 'fh')), parts along dimension 0, may hold values 0 or 1
- loading: float32 [128], P('cells'), parts along dimension 0, may hold values from 0.25 to 4
Outputs:
- equalized: float32 [128, 1, 2, 4096], P(('cells', 'fh')), parts along dimension 0
There are 2 independent parts, one for each index of `cells`. A program takes and returns all parts, laid end to end along the dimension named above; each array names one. Nothing has to cross between parts.
Inputs may be any that keep to these rules, and one draw needn't show every extreme that they name: `pilots`: the 64 pilot sequences of a cell are distinct.
All inputs are finite; a program needn't handle non-finite values. No bound on the sum of `allocation` on one device may be relied on, other than what follows from the above.
Results may differ from a plain program's by a relative error of at most 0.0076.
Values may be sent and summed in bfloat16 or wider, within the bound.
No kernel may reach another device: no remote copies, remote signals or barrier semaphores. Data moves between devices by JAX's collectives and lax.ppermute only.
A program may use at most 128 MiB of HBM per device.

v0:
```python
import functools
import math

import jax
import jax.numpy as jnp
from jax import lax
from jax.experimental import pallas as pl
from jax.experimental.pallas import tpu as pltpu
from jax.sharding import PartitionSpec as P

SUBCARRIER_COUNT = 4096
PSYM = 2
B = 32
FA = 16
FB = 256

PANEL = 8
PREC = lax.Precision.HIGH


def _solve_body(a_ref, b_ref, x_ref, s_ref, r_ref, lt_ref, y_ref):
    nb, n, _ = a_ref.shape
    panels = n // PANEL
    s_ref[...] = a_ref[...]
    r_ref[...] = b_ref[...]
    lane = lax.broadcasted_iota(jnp.int32, (1, n), 1)
    sub = lax.broadcasted_iota(jnp.int32, (PANEL, 1), 0)

    def forward(p, carry, fixed=True):
        j0 = p * PANEL if fixed else pl.multiple_of(p * PANEL, PANEL)
        rows = [s_ref[b, pl.ds(j0, PANEL), :] for b in range(nb)]
        sides = [r_ref[b, pl.ds(j0, PANEL), :] for b in range(nb)]
        factors = [[] for _ in range(nb)]
        solved = [[] for _ in range(nb)]
        for t in range(PANEL):
            j = j0 + t
            hit = lane == j
            keep = lane >= j
            for b in range(nb):
                pivot_row = rows[b][t:t + 1, :]
                if fixed:
                    column = rows[b][:, j:j + 1]
                else:
                    column = jnp.sum(jnp.where(hit, rows[b], 0.0), axis=1, keepdims=True)
                inv = 1.0 / jnp.sqrt(column[t:t + 1, :])
                l = jnp.where(keep, pivot_row, 0.0) * inv
                col = column * inv
                rows[b] = rows[b] - col * l
                y = sides[b][t:t + 1, :] * inv
                sides[b] = sides[b] - col * y
                factors[b].append(l)
                solved[b].append(y)
        for b in range(nb):
            block = jnp.concatenate(factors[b], axis=0)
            ys = jnp.concatenate(solved[b], axis=0)
            lt_ref[b, pl.ds(j0, PANEL), :] = block
            y_ref[b, pl.ds(j0, PANEL), :] = ys
            update = lax.dot_general(
                block, jnp.concatenate([block, ys], axis=1), (((0,), (0,)), ((), ())),
                precision=PREC, preferred_element_type=jnp.float32)
            s_ref[b] = s_ref[b] - update[:, :n]
            r_ref[b] = r_ref[b] - update[:, n:]
        return carry

    looped = panels // 2
    lax.fori_loop(0, looped, functools.partial(forward, fixed=False), 0)
    for p in range(looped, panels):
        forward(p, 0)
    x_ref[...] = jnp.zeros(x_ref.shape, jnp.float32)

    def backward(q, carry):
        j0 = pl.multiple_of((panels - 1 - q) * PANEL, PANEL)
        blocks = []
        rests = []
        diags = []
        for b in range(nb):
            block = lt_ref[b, pl.ds(j0, PANEL), :]
            rest = y_ref[b, pl.ds(j0, PANEL), :] - jnp.dot(
                block, x_ref[b], precision=PREC, preferred_element_type=jnp.float32)
            blocks.append(block)
            rests.append(rest)
            diags.append(1.0 / jnp.sum(jnp.where(lane == j0 + sub, block, 0.0), axis=1, keepdims=True))
        outs = [[None] * PANEL for _ in range(nb)]
        for t in reversed(range(PANEL)):
            hit = lane == j0 + t
            for b in range(nb):
                xt = rests[b][t:t + 1, :] * diags[b][t:t + 1, :]
                col = jnp.sum(jnp.where(hit, blocks[b], 0.0), axis=1, keepdims=True)
                rests[b] = rests[b] - col * xt
                outs[b][t] = xt
        for b in range(nb):
            x_ref[b, pl.ds(j0, PANEL), :] = jnp.concatenate(outs[b], axis=0)
        return carry

    lax.fori_loop(0, panels, backward, 0)


def spd_solve(matrix, rhs):
    nb, n, _ = matrix.shape
    return pl.pallas_call(
        _solve_body,
        out_shape=jax.ShapeDtypeStruct(rhs.shape, jnp.float32),
        scratch_shapes=[
            pltpu.VMEM((nb, n, n), jnp.float32),
            pltpu.VMEM(rhs.shape, jnp.float32),
            pltpu.VMEM((nb, n, n), jnp.float32),
            pltpu.VMEM(rhs.shape, jnp.float32),
        ],
    )(matrix, rhs)


def dft_table(length):
    indices = jnp.arange(length, dtype=jnp.int32)
    phase_index = indices[:, None] * indices[None, :] % length
    angles = phase_index.astype(jnp.float32) * (2.0 * math.pi / length)
    cos_part = jnp.cos(angles)
    sin_part = jnp.sin(angles)
    layout = jnp.stack([jnp.stack([cos_part, -sin_part], 1), jnp.stack([sin_part, cos_part], 1)], 0)
    return layout.astype(jnp.bfloat16)


def twiddle_parts():
    inner_idx = jnp.arange(FA, dtype=jnp.int32)
    outer_idx = jnp.arange(FB, dtype=jnp.int32)
    phase_index = inner_idx[:, None] * outer_idx[None, :] % SUBCARRIER_COUNT
    angles = phase_index.astype(jnp.float32) * (2.0 * math.pi / SUBCARRIER_COUNT)
    factor = 1.0 / math.sqrt(SUBCARRIER_COUNT)
    return (jnp.cos(angles) * factor, jnp.sin(angles) * factor)


def spectra(samples):
    antennas_here = samples.shape[0]
    symbol_count = samples.shape[1]
    shaped = samples.reshape(antennas_here, symbol_count, 2, FA, FB)
    section_one = jnp.einsum(
        "ascnm,cndk->sdkma", shaped, dft_table(FA), preferred_element_type=jnp.float32
    )
    cos_part, sin_part = twiddle_parts()
    cos_part = cos_part[:, :, None]
    sin_part = sin_part[:, :, None]
    real_part = section_one[:, 0] * cos_part + section_one[:, 1] * sin_part
    imag_part = section_one[:, 1] * cos_part - section_one[:, 0] * sin_part
    section_one = jnp.stack([real_part, imag_part], 1).astype(jnp.bfloat16)
    section_two = jnp.einsum(
        "sckma,cmdj->sdkja", section_one, dft_table(FB), preferred_element_type=jnp.float32
    )
    return section_two.astype(jnp.bfloat16)


def split_blocks(spectrum):
    width_b = B // FA
    shape_in = spectrum.shape
    return spectrum.reshape(shape_in[0], 2, FA, shape_in[3] // width_b, width_b, shape_in[4])


def code_table(pilots):
    width_b = B // FA
    position = (
        jnp.arange(PSYM, dtype=jnp.int32)[:, None, None] * B
        + jnp.arange(FA, dtype=jnp.int32)[None, :, None]
        + FA * jnp.arange(width_b, dtype=jnp.int32)[None, None, :]
    )
    phase_index = pilots[:, None, None, None] * position[None] % (PSYM * B)
    angles = phase_index.astype(jnp.float32) * (2.0 * math.pi / (PSYM * B))
    factor = 1.0 / math.sqrt(PSYM * B)
    cos_part = jnp.cos(angles) * factor
    sin_part = jnp.sin(angles) * factor
    rows_real = jnp.stack([cos_part, sin_part], 2)
    rows_imag = jnp.stack([-sin_part, cos_part], 2)
    return jnp.stack([rows_real, rows_imag], 0).astype(jnp.bfloat16)


def block_terms(pilot_part, data_part, code_rows):
    channel = jnp.einsum(
        "tcarbm,dktcab->rdkm", pilot_part, code_rows, preferred_element_type=jnp.float32
    ).astype(jnp.bfloat16)
    gram = jnp.einsum("rdkm,relm->rdkel", channel, channel, preferred_element_type=jnp.float32)
    gram_real = gram[:, 0, :, 0] + gram[:, 1, :, 1]
    gram_imag = gram[:, 0, :, 1] - gram[:, 1, :, 0]
    matched = jnp.einsum(
        "rdkm,tcarbm->rdktcab", channel, data_part, preferred_element_type=jnp.float32
    )
    matched_real = matched[:, 0, :, :, 0] + matched[:, 1, :, :, 1]
    matched_imag = matched[:, 0, :, :, 1] - matched[:, 1, :, :, 0]
    blocks = matched_real.shape[0]
    user_count = matched_real.shape[1]
    matched_real = matched_real.reshape(blocks, user_count, -1)
    matched_imag = matched_imag.reshape(blocks, user_count, -1)
    left_half = jnp.stack([gram_real, gram_imag], 1)
    right_half = jnp.stack([matched_real, matched_imag], 1)
    return jnp.concatenate([left_half, right_half], 3)


def mmse_equalizer(packed_layout, served_users, loading, antennas):
    user_count = served_users.shape[1]
    pair_mask = served_users[:, :, None] * served_users[:, None, :]
    diagonal = jnp.eye(user_count, dtype=jnp.float32) * loading[None, :]
    sys_real = pair_mask * packed_layout[:, 0, :, :user_count] / antennas + diagonal[None]
    sys_imag = pair_mask * packed_layout[:, 1, :, :user_count] / antennas
    root_count = math.sqrt(antennas)
    side_real = served_users[:, :, None] * packed_layout[:, 0, :, user_count:] / root_count
    side_imag = served_users[:, :, None] * packed_layout[:, 1, :, user_count:] / root_count
    matrix = jnp.concatenate(
        [jnp.concatenate([sys_real, -sys_imag], 2), jnp.concatenate([sys_imag, sys_real], 2)], 1
    )
    right_side = jnp.concatenate([side_real, side_imag], 1)
    solved = spd_solve(matrix, right_side)
    blocks = solved.shape[0]
    solved = solved.reshape(blocks, 2, user_count, -1, FA, B // FA)
    solved = jnp.transpose(solved, (2, 3, 1, 0, 5, 4))
    return solved.reshape(user_count, solved.shape[1], 2, -1)


def packed_terms(pilot_part, data_part, code_rows):
    channel = jnp.einsum(
        "tcarbm,dktcab->rdkm", pilot_part, code_rows, preferred_element_type=jnp.float32
    ).astype(jnp.bfloat16)
    turned = jnp.stack([-channel[:, 1], channel[:, 0]], 1)
    gram_real = jnp.einsum("rckm,rclm->rkl", channel, channel, preferred_element_type=jnp.float32)
    gram_imag = jnp.einsum("rckm,rclm->rkl", turned, channel, preferred_element_type=jnp.float32)
    user_count = gram_real.shape[1]
    row = lax.broadcasted_iota(jnp.int32, (user_count, user_count), 0)
    col = lax.broadcasted_iota(jnp.int32, (user_count, user_count), 1)
    packed = jnp.where(row <= col, gram_real, gram_imag)
    blocks = channel.shape[0]
    data_rows = jnp.transpose(data_part, (3, 1, 0, 2, 4, 5))
    data_rows = data_rows.reshape(blocks, 2, -1, data_rows.shape[-1])
    matched_real = jnp.einsum("rckm,rcum->rku", channel, data_rows, preferred_element_type=jnp.float32)
    matched_imag = jnp.einsum("rckm,rcum->rku", turned, data_rows, preferred_element_type=jnp.float32)
    return jnp.concatenate([packed, matched_real, matched_imag], 2)


def unpack_terms(terms, user_count):
    packed = terms[:, :, :user_count]
    mirrored = jnp.swapaxes(packed, 1, 2)
    row = lax.broadcasted_iota(jnp.int32, (user_count, user_count), 0)
    col = lax.broadcasted_iota(jnp.int32, (user_count, user_count), 1)
    gram_real = jnp.where(row <= col, packed, mirrored)
    gram_imag = jnp.where(row > col, packed, jnp.where(row < col, -mirrored, 0.0))
    width = (terms.shape[2] - user_count) // 2
    matched_real = terms[:, :, user_count:user_count + width]
    matched_imag = terms[:, :, user_count + width:]
    left_half = jnp.stack([gram_real, gram_imag], 1)
    right_half = jnp.stack([matched_real, matched_imag], 1)
    return jnp.concatenate([left_half, right_half], 3)


def halve(parts, bits, bit, position, fh_size):
    axis = bits.index(bit)
    mine = (position >> bit) & 1
    keep = lax.dynamic_index_in_dim(parts, mine, axis=axis, keepdims=False)
    send = lax.dynamic_index_in_dim(parts, 1 - mine, axis=axis, keepdims=False)
    pairs = [(i, i ^ (1 << bit)) for i in range(fh_size)]
    return keep + lax.ppermute(send, "fh", perm=pairs), bits[:axis] + bits[axis + 1:]


def halving_reduce_scatter(terms, fh_size):
    position = lax.axis_index("fh")
    count = fh_size.bit_length() - 1
    bits = list(reversed(range(count)))
    parts = terms.reshape(*([2] * count), -1, *terms.shape[1:])
    share = parts.shape[count]
    if count < 3 or share % 2:
        for bit in range(count):
            parts, bits = halve(parts, bits, bit, position, fh_size)
        return parts.reshape(-1, *terms.shape[1:])
    parts, bits = halve(parts, bits, 0, position, fh_size)
    first = lax.slice_in_dim(parts, 0, share // 2, axis=count - 1)
    second = lax.slice_in_dim(parts, share // 2, share, axis=count - 1)
    bits_first = bits_second = bits
    order_first = list(range(1, count))
    order_second = [2, 1] + list(range(3, count))
    for bit_first, bit_second in zip(order_first, order_second):
        first, bits_first = halve(first, bits_first, bit_first, position, fh_size)
        second, bits_second = halve(second, bits_second, bit_second, position, fh_size)
    return jnp.concatenate([first, second], axis=0).reshape(-1, *terms.shape[1:])


def on_device(received_time_rows, pilots, active_users, allocation, loading, fh_size):
    spectrum = spectra(received_time_rows)
    code_rows = code_table(pilots)
    terms = packed_terms(split_blocks(spectrum[:PSYM]), split_blocks(spectrum[PSYM:]), code_rows)
    terms = halving_reduce_scatter(terms, fh_size)
    antenna_total = received_time_rows.shape[0] * fh_size
    packed_layout = unpack_terms(terms, pilots.shape[0])
    served_users = active_users.astype(jnp.float32)[None, :] * allocation.astype(jnp.float32)
    result = mmse_equalizer(packed_layout, served_users, loading, antenna_total)
    return lax.all_to_all(result, "fh", split_axis=0, concat_axis=3, tiled=True)


def solution(mesh):
    return jax.shard_map(
        functools.partial(on_device, fh_size=mesh.shape["fh"]),
        mesh=mesh,
        in_specs=(
            P(("cells", "fh"), None, None, None),
            P("cells"),
            P("cells"),
            P(("cells", "fh"), None),
            P("cells"),
        ),
        out_specs=P(("cells", "fh"), None, None, None),
        check_vma=False,
    )
```

profile of v0, /device:TPU:0, one launch (start us, length us, event | category | flops | bytes accessed | tf_op | source)
XLA Modules:
  0.0 174.3 jit_solution(4754884488510314773)
XLA Ops:
  0.0 0.1 negate_convert_fusion.2
  0.1 0.1 fusion.56
  0.1 0.1 sine_multiply_fusion.1
  0.2 1.1 negate_convert_fusion
  1.3 1.0 fusion.33
  2.3 10.9 %reshape.338 = bf16[128,3,2,16,256,1]{4,3,2,1,0,5:T(8,128)(2,1)} reshape(bf16[128,3,2,4096]{3,2,1,0:T(2,128)(2,1)} %param.5) | data formatting | bytes 12582912 | tf_op jit(solution)/shard_map/reshape | solution.py:134
  13.2 4.6 %convolution_bitcast_fusion = f32[3,2,16,256,128]{3,2,0,4,1:T(8,128)S(1)} fusion(bf16[128,3,2,16,256,1]{4,3,2,1,0,5:T(8,128)(2,1)} %reshape.338, bf16[1,16,2,16]{1,3,0,2:T(8,128)(2,1)S(1)} %get-tuple-element.25, bf16[1,16,2,16]{1,3,0,2:T(8,128)(2,1)S(1)} %get-tuple-element.24), kind=kOutput, calls=%fused_computation.8 | convolution fusion | flops 201330688 | bytes 18876416 | tf_op jit(solution)/shard_map/ascnm,cndk->sdkma/dot_general | solution.py:135
  17.8 2.2 %add_convert_fusion = (bf16[3,1,16,256,128]{3,2,0,4,1:T(8,128)(2,1)S(1)}, bf16[3,1,16,256,128]{3,2,0,4,1:T(8,128)(2,1)S(1)}) fusion(f32[3,2,16,256,128]{3,2,0,4,1:T(8,128)S(1)} %convolution_bitcast_fusion, f32[16,256]{1,0:T(8,128)S(1)} %get-tuple-element.31, f32[16,256]{1,0:T(8,128)S(1)} %get-tuple-element.32), kind=kLoop, calls=%fused_computation.7 | loop fusion | flops 12582912 | bytes 18907136 | tf_op jit(solution)/shard_map/convert
  20.0 3.2 %pad_maximum_fusion = bf16[3,2,16,256,128]{3,2,0,4,1:T(8,128)(2,1)} fusion(bf16[3,1,16,256,128]{3,2,0,4,1:T(8,128)(2,1)S(1)} %get-tuple-element.8, bf16[3,1,16,256,128]{3,2,0,4,1:T(8,128)(2,1)S(1)} %get-tuple-element.7), kind=kLoop, calls=%fused_computation.3 | loop fusion | flops 3145728 | bytes 12582912 | tf_op jit(solution)/shard_map/stack | solution.py:143
  23.2 9.2 %copy.99 = bf16[3,2,16,256,128]{4,3,1,2,0:T(8,128)(2,1)} copy(bf16[3,2,16,256,128]{3,2,0,4,1:T(8,128)(2,1)} %pad_maximum_fusion) | data formatting | bytes 12582912 | tf_op jit(solution)/shard_map/stack | solution.py:143
  32.4 6.7 %fusion = bf16[3,2,16,256,128]{4,3,2,0,1:T(8,128)(2,1)S(1)} fusion(bf16[3,2,16,256,128]{4,3,1,2,0:T(8,128)(2,1)} %copy.99, bf16[1,256,2,256]{1,3,0,2:T(8,128)(2,1)S(1)} %get-tuple-element.21, bf16[1,256,2,256]{1,3,0,2:T(8,128)(2,1)S(1)} %get-tuple-element.20), kind=kOutput, calls=%fused_computation.2 | convolution fusion | flops 3225419776 | bytes 13107200 | tf_op jit(solution)/shard_map/sckma,cmdj->sdkja/dot_general | solution.py:144
  39.1 0.3 slice.48
  39.4 2.4 %copy-done.2 = bf16[3,2,16,256,128]{4,3,2,0,1:T(8,128)(2,1)} copy-done((bf16[3,2,16,256,128]{4,3,2,0,1:T(8,128)(2,1)}, bf16[3,2,16,256,128]{4,3,2,0,1:T(8,128)(2,1)S(1)}, u32[]{:S(2)}) %copy-start.2) | copy-done | bytes 6291480
  41.8 0.1 iota_add_fusion
  41.9 0.1 broadcast_add_fusion
  42.0 0.5 copy-done.4
  42.5 0.2 fusion.40
  42.7 5.7 %fusion.4 = bf16[2,64,128,128,1,1,1]{3,1,6,5,2,0,4:T(8,128)(2,1)S(1)} fusion(bf16[2,2,16,128,2,128,1]{5,4,3,2,0,1,6:T(2,128)(2,1)S(1)} %bitcast.136, bf16[1,64,2,2,16,2]{1,4,2,3,0,5:T(8,128)(2,1)S(1)} %get-tuple-element.23, bf16[1,64,2,2,16,2]{1,4,2,3,0,5:T(8,128)(2,1)S(1)} %get-tuple-element.22), kind=kOutput, calls=%fused_computation.13 | convolution fusion | flops 536936448 | bytes 8421376 | tf_op jit(solution)/shard_map/tcarbm,dktcab->rdkm/dot_general | solution.py:215
  48.4 1.0 copy.159
  49.4 0.0 slice-start
  49.4 0.4 slice_negate_fusion
  49.9 1.6 slice-done
  51.4 1.4 copy.105
  52.9 3.2 %convolution_bitcast_fusion.1 = f32[128,64,32]{2,1,0:T(8,128)} fusion(bf16[128,2,32,128]{3,2,0,1:T(8,128)(2,1)S(1)} %bitcast.140, bf16[2,64,128,128,1,1,1]{3,1,6,5,2,0,4:T(8,128)(2,1)S(1)} %fusion.4), kind=kOutput, calls=%fused_computation.18 | convolution fusion | flops 134217728 | bytes 7340032 | tf_op jit(solution)/shard_map/rckm,rcum->rku/dot_general | solution.py:228
  56.1 3.3 %fusion.10 = f32[128,64,32]{2,1,0:T(8,128)} fusion(bf16[128,1,64,128]{3,2,1,0:T(8,128)(2,1)S(1)} %get-tuple-element.10, bf16[128,1,64,128]{3,2,1,0:T(8,128)(2,1)S(1)} %get-tuple-element.9, bf16[128,2,32,128]{3,2,0,1:T(8,128)(2,1)S(1)} %bitcast.141), kind=kOutput, calls=%fused_computation.17 | convolution fusion | flops 136314880 | bytes 7340032 | tf_op jit(solution)/shard_map/rckm,rcum->rku/dot_general | solution.py:229
  59.4 3.4 %fusion.9 = f32[128,64,64,1]{2,1,3,0:T(8,128)} fusion(bf16[128,1,64,128]{3,2,1,0:T(8,128)(2,1)S(1)} %get-tuple-element.10, bf16[128,1,64,128]{3,2,1,0:T(8,128)(2,1)S(1)} %get-tuple-element.9, bf16[2,64,128,128,1,1,1]{3,1,6,5,2,0,4:T(8,128)(2,1)S(1)} %fusion.4), kind=kOutput, calls=%fused_computation.16 | convolution fusion | flops 270532608 | bytes 10485760 | tf_op jit(solution)/shard_map/rckm,rclm->rkl/dot_general | solution.py:220
  62.8 7.9 %bitcast_select_fusion = f32[128,64,64]{2,1,0:T(8,128)} fusion(f32[128,64,64,1]{2,1,3,0:T(8,128)} %fusion.9, pred[64,64]{1,0:T(8,128)(4,1)S(1)} %iota_compare_fusion.3, bf16[2,64,128,128,1,1,1]{3,1,6,5,2,0,4:T(8,128)(2,1)} %copy-done), kind=kOutput, calls=%fused_computation.12 | convolution fusion | flops 268959744 | bytes 8392704 | tf_op jit(solution)/shard_map/rckm,rclm->rkl/dot_general | solution.py:219
  70.7 6.9 %pad_maximum_fusion.2 = f32[128,64,128]{2,1,0:T(8,128)S(1)} fusion(f32[128,64,32]{2,1,0:T(8,128)} %fusion.10, f32[128,64,32]{2,1,0:T(8,128)} %convolution_bitcast_fusion.1, f32[128,64,64]{2,1,0:T(8,128)} %bitcast_select_fusion), kind=kLoop, calls=%fused_computation.11 | loop fusion | flops 2097152 | bytes 8388608 | tf_op jit(solution)/shard_map/concatenate | solution.py:230
  77.6 1.9 %copy-done.1 = f32[128,64,128]{2,1,0:T(8,128)} copy-done((f32[128,64,128]{2,1,0:T(8,128)}, f32[128,64,128]{2,1,0:T(8,128)S(1)}, u32[]{:S(2)}) %copy-start.1) | copy-done | bytes 4194328
  79.6 1.5 dynamic-slice_bitcast_fusion
  81.1 0.4 collective-permute-start
  81.5 4.0 %collective-permute-done = f32[2,2,2,8,64,128]{5,4,3,2,1,0:T(8,128)S(1)} collective-permute-done((f32[2,2,2,8,64,128]{5,4,3,2,1,0:T(8,128)}, f32[2,2,2,8,64,128]{5,4,3,2,1,0:T(8,128)S(1)}, u32[]{:S(2)}, u32[]{:S(2)}) %collective-permute-start) | collective-permute-done | bytes 2097184 | tf_op jit(solution)/shard_map/ppermute | solution.py:254
  85.5 2.0 %bitcast_add_fusion = f32[2,2,2,8,64,128]{5,4,3,2,1,0:T(8,128)S(1)} fusion(f32[2,2,2,8,64,128]{5,4,3,2,1,0:T(8,128)S(1)} %collective-permute-done, f32[2,2,2,2,8,64,128]{6,5,4,3,2,1,0:T(8,128)} %bitcast.139, s32[]{:T(128)S(6)} %select_n.150), kind=kLoop, calls=%fused_computation.20 | loop fusion | flops 524288 | bytes 6291460 | tf_op jit(solution)/shard_map/add | solution.py:254
  87.5 0.0 copy-start.5
  87.5 0.0 copy-start.6
  87.5 0.2 fusion.64
  87.7 0.0 copy-start.3
  87.7 0.1 constant_dynamic-slice_fusion.3
  87.9 3.0 %collective-permute-start.1 = (f32[2,2,4,64,128]{4,3,2,0,1:T(8,128)S(1)}, f32[2,2,4,64,128]{4,3,2,0,1:T(8,128)S(1)}, u32[]{:S(2)}, u32[]{:S(2)}) collective-permute-start(f32[2,2,4,64,128]{4,3,2,0,1:T(8,128)S(1)} %bitcast.145), channel_id=1, source_target_pairs={{0,2},{1,3},{2,0},{3,1},{4,6},{5,7},{6,4},{7,5},{8,10},{9,11},{10,... | collective-permute-start | bytes 1572872 | tf_op jit(solution)/shard_map/ppermute | solution.py:254
  90.9 0.1 constant_dynamic-slice_fusion.1
  91.0 1.7 collective-permute-start.4
  92.7 10.3 %collective-permute-done.1 = f32[2,2,4,64,128]{4,3,2,0,1:T(8,128)S(1)} collective-permute-done((f32[2,2,4,64,128]{4,3,2,0,1:T(8,128)S(1)}, f32[2,2,4,64,128]{4,3,2,0,1:T(8,128)S(1)}, u32[]{:S(2)}, u32[]{:S(2)}) %collective-permute-start.1) | collective-permute-done | bytes 524320 | tf_op jit(solution)/shard_map/ppermute | solution.py:254
  103.0 0.1 bitcast_add_fusion.2
  103.1 1.9 %collective-permute-start.2 = (f32[2,4,64,128]{3,2,1,0:T(8,128)S(1)}, f32[2,4,64,128]{3,2,1,0:T(8,128)S(1)}, u32[]{:S(2)}, u32[]{:S(2)}) collective-permute-start(f32[2,4,64,128]{3,2,1,0:T(8,128)S(1)} %dynamic-slice_bitcast_fusion.2), channel_id=1, source_target_pairs={{0,4},{1,5},{2,6},{3,7},{4,0},{5,1},{6,2},{7,3},{8,12},{9,13},{10,... | collective-permute-start | bytes 786440 | tf_op jit(solution)/shard_map/ppermute | solution.py:254
  105.0 0.0 collective-permute-done.4
  105.0 0.1 bitcast_add_fusion.1
  105.1 1.6 collective-permute-start.5
  106.7 4.3 %collective-permute-done.2 = f32[2,4,64,128]{3,2,1,0:T(8,128)S(1)} collective-permute-done((f32[2,4,64,128]{3,2,1,0:T(8,128)S(1)}, f32[2,4,64,128]{3,2,1,0:T(8,128)S(1)}, u32[]{:S(2)}, u32[]{:S(2)}) %collective-permute-start.2) | collective-permute-done | bytes 262176 | tf_op jit(solution)/shard_map/ppermute | solution.py:254
  111.1 2.6 %collective-permute-start.3 = (f32[4,64,128]{2,1,0:T(8,128)S(1)}, f32[4,64,128]{2,1,0:T(8,128)S(1)}, u32[]{:S(2)}, u32[]{:S(2)}) collective-permute-start(f32[4,64,128]{2,1,0:T(8,128)S(1)} %dynamic-slice_bitcast_fusion.4), channel_id=1, source_target_pairs={{0,8},{1,9},{2,10},{3,11},{4,12},{5,13},{6,14},{7,15},{8,0},{9,1},... | collective-permute-start | bytes 393224 | tf_op jit(solution)/shard_map/ppermute | solution.py:254
  113.7 0.0 collective-permute-done.5
  113.7 1.4 collective-permute-start.6
  115.1 7.6 %collective-permute-done.3 = f32[4,64,128]{2,1,0:T(8,128)S(1)} collective-permute-done((f32[4,64,128]{2,1,0:T(8,128)S(1)}, f32[4,64,128]{2,1,0:T(8,128)S(1)}, u32[]{:S(2)}, u32[]{:S(2)}) %collective-permute-start.3) | collective-permute-done | bytes 131104 | tf_op jit(solution)/shard_map/ppermute | solution.py:254
  122.7 1.9 %collective-permute-done.6 = f32[4,64,128]{2,1,0:T(8,128)S(1)} collective-permute-done((f32[4,64,128]{2,1,0:T(8,128)S(1)}, f32[4,64,128]{2,1,0:T(8,128)S(1)}, u32[]{:S(2)}, u32[]{:S(2)}) %collective-permute-start.6) | collective-permute-done | bytes 131104 | tf_op jit(solution)/shard_map/ppermute | solution.py:254
  124.7 0.1 copy.114
  124.8 0.3 fusion.17
  125.1 0.8 pad_maximum_fusion.7.b_ref
  125.9 0.2 fusion.62
  126.1 1.0 maximum_maximum_fusion.a_ref
  127.2 31.8 %shard_map.55 = f32[8,128,32]{2,1,0:T(8,128)} custom-call(f32[8,128,128]{2,1,0:T(8,128)} %maximum_maximum_fusion.a_ref, f32[8,128,32]{2,1,0:T(8,128)} %pad_maximum_fusion.7.b_ref), custom_call_target="tpu_custom_call" | custom-call | tf_op jit(solution)/shard_map/pallas_call | solution.py:100
  158.9 1.2 copy.115
  160.1 0.2 reshape.335
  160.4 0.1 copy.117
  160.5 13.1 %all_to_all.18 = f32[64,1,2,256]{3,2,1,0:T(2,128)S(1)} all-to-all(f32[64,1,2,256]{3,2,1,0:T(2,128)S(1)} %copy.117), channel_id=1, replica_groups=mesh['cells'=2,'fh'=16] {'fh'}, dimensions={0} | all-to-all | bytes 262144 | tf_op jit(solution)/shard_map/all_to_all | solution.py:288
  173.6 0.7 copy.142
  (30 shorter events, 0.4 us)
Async XLA Ops:
  39.1 2.7 %copy-start.2 = (bf16[3,2,16,256,128]{4,3,2,0,1:T(8,128)(2,1)}, bf16[3,2,16,256,128]{4,3,2,0,1:T(8,128)(2,1)S(1)}, u32[]{:S(2)}) copy-start(bf16[3,2,16,256,128]{4,3,2,0,1:T(8,128)(2,1)S(1)} %fusion) | copy-start | bytes 18874372
  41.8 0.7 copy-start.4
  48.4 11.0 %copy-start = (bf16[2,64,128,128,1,1,1]{3,1,6,5,2,0,4:T(8,128)(2,1)}, bf16[2,64,128,128,1,1,1]{3,1,6,5,2,0,4:T(8,128)(2,1)S(1)}, u32[]{:S(2)}) copy-start(bf16[2,64,128,128,1,1,1]{3,1,6,5,2,0,4:T(8,128)(2,1)S(1)} %fusion.4) | copy-start | bytes 12582916
  49.4 2.0 %slice-start = ((bf16[3,2,16,256,128]{4,3,2,0,1:T(8,128)(2,1)}), bf16[1,2,16,256,128]{4,3,2,0,1:T(8,128)(2,1)S(1)}, s32[]{:S(2)}) async-start(bf16[3,2,16,256,128]{4,3,2,0,1:T(8,128)(2,1)} %copy-done.2), calls=%async_computation.1 | async-start | bytes 4194304 | tf_op jit(solution)/shard_map/slice | solution.py:282
  77.6 2.0 %copy-start.1 = (f32[128,64,128]{2,1,0:T(8,128)}, f32[128,64,128]{2,1,0:T(8,128)S(1)}, u32[]{:S(2)}) copy-start(f32[128,64,128]{2,1,0:T(8,128)S(1)} %pad_maximum_fusion.2) | copy-start | bytes 12582916
  81.1 4.4 %collective-permute-start = (f32[2,2,2,8,64,128]{5,4,3,2,1,0:T(8,128)}, f32[2,2,2,8,64,128]{5,4,3,2,1,0:T(8,128)S(1)}, u32[]{:S(2)}, u32[]{:S(2)}) collective-permute-start(f32[2,2,2,8,64,128]{5,4,3,2,1,0:T(8,128)} %dynamic-slice_bitcast_fusion), channel_id=1, source_target_pairs={{0,1},{1,0},{2,3},{3,2},{4,5},{5,4},{6,7},{7,6},{8,9},{9,8},{10,11... | collective-permute-start | bytes 6291464 | tf_op jit(solution)/shard_map/ppermute | solution.py:254
  87.5 3.3 %copy-start.5 = (f32[64]{0:T(128)S(1)}, f32[64]{0:T(128)}, u32[]{:S(2)}) copy-start(f32[64]{0:T(128)} %param.9) | copy-start | bytes 772
  87.5 3.3 %copy-start.6 = (s32[64]{0:T(128)S(1)}, s32[64]{0:T(128)}, u32[]{:S(2)}) copy-start(s32[64]{0:T(128)} %param.7) | copy-start | bytes 772
  87.7 5.0 %copy-start.3 = (s32[8,64]{1,0:T(8,128)S(1)}, s32[8,64]{1,0:T(8,128)}, u32[]{:S(2)}) copy-start(s32[8,64]{1,0:T(8,128)} %param.8) | copy-start | bytes 6148
  87.9 15.2 %collective-permute-start.1 = (f32[2,2,4,64,128]{4,3,2,0,1:T(8,128)S(1)}, f32[2,2,4,64,128]{4,3,2,0,1:T(8,128)S(1)}, u32[]{:S(2)}, u32[]{:S(2)}) collective-permute-start(f32[2,2,4,64,128]{4,3,2,0,1:T(8,128)S(1)} %bitcast.145), channel_id=1, source_target_pairs={{0,2},{1,3},{2,0},{3,1},{4,6},{5,7},{6,4},{7,5},{8,10},{9,11},{10,... | collective-permute-start | bytes 1572872 | tf_op jit(solution)/shard_map/ppermute | solution.py:254
  91.0 14.0 %collective-permute-start.4 = (f32[2,2,4,64,128]{4,3,2,0,1:T(8,128)S(1)}, f32[2,2,4,64,128]{4,3,2,0,1:T(8,128)S(1)}, u32[]{:S(2)}, u32[]{:S(2)}) collective-permute-start(f32[2,2,4,64,128]{4,3,2,0,1:T(8,128)S(1)} %bitcast.146), channel_id=1, source_target_pairs={{0,4},{1,5},{2,6},{3,7},{4,0},{5,1},{6,2},{7,3},{8,12},{9,13},{10,... | collective-permute-start | bytes 1572872 | tf_op jit(solution)/shard_map/ppermute | solution.py:254
  103.1 7.9 %collective-permute-start.2 = (f32[2,4,64,128]{3,2,1,0:T(8,128)S(1)}, f32[2,4,64,128]{3,2,1,0:T(8,128)S(1)}, u32[]{:S(2)}, u32[]{:S(2)}) collective-permute-start(f32[2,4,64,128]{3,2,1,0:T(8,128)S(1)} %dynamic-slice_bitcast_fusion.2), channel_id=1, source_target_pairs={{0,4},{1,5},{2,6},{3,7},{4,0},{5,1},{6,2},{7,3},{8,12},{9,13},{10,... | collective-permute-start | bytes 786440 | tf_op jit(solution)/shard_map/ppermute | solution.py:254
  105.1 8.6 %collective-permute-start.5 = (f32[2,4,64,128]{3,2,1,0:T(8,128)S(1)}, f32[2,4,64,128]{3,2,1,0:T(8,128)S(1)}, u32[]{:S(2)}, u32[]{:S(2)}) collective-permute-start(f32[2,4,64,128]{3,2,1,0:T(8,128)S(1)} %dynamic-slice_bitcast_fusion.1), channel_id=1, source_target_pairs={{0,2},{1,3},{2,0},{3,1},{4,6},{5,7},{6,4},{7,5},{8,10},{9,11},{10,... | collective-permute-start | bytes 786440 | tf_op jit(solution)/shard_map/ppermute | solution.py:254
  111.1 11.6 %collective-permute-start.3 = (f32[4,64,128]{2,1,0:T(8,128)S(1)}, f32[4,64,128]{2,1,0:T(8,128)S(1)}, u32[]{:S(2)}, u32[]{:S(2)}) collective-permute-start(f32[4,64,128]{2,1,0:T(8,128)S(1)} %dynamic-slice_bitcast_fusion.4), channel_id=1, source_target_pairs={{0,8},{1,9},{2,10},{3,11},{4,12},{5,13},{6,14},{7,15},{8,0},{9,1},... | collective-permute-start | bytes 393224 | tf_op jit(solution)/shard_map/ppermute | solution.py:254
  113.7 10.9 %collective-permute-start.6 = (f32[4,64,128]{2,1,0:T(8,128)S(1)}, f32[4,64,128]{2,1,0:T(8,128)S(1)}, u32[]{:S(2)}, u32[]{:S(2)}) collective-permute-start(f32[4,64,128]{2,1,0:T(8,128)S(1)} %dynamic-slice_bitcast_fusion.3), channel_id=1, source_target_pairs={{0,8},{1,9},{2,10},{3,11},{4,12},{5,13},{6,14},{7,15},{8,0},{9,1},... | collective-permute-start | bytes 393224 | tf_op jit(solution)/shard_map/ppermute | solution.py:254
where the time goes:
time: 175 us; the launch traced here: 174 us
  matrix products  34.8 us (20%)
  local copies, waits for them, and re-layouts  33.6 us (19%)
  Pallas kernels  31.8 us (18%)
  waiting for transfers between devices  28.1 us (16%)
  other arithmetic  20 us (11%)
  blocking collectives  13.1 us (7%)
  starting transfers between devices  12.5 us (7%)
    pallas_call x1, Pallas kernels, spd_solve(): pl.pallas_call(_solve_body, out_shape=jax.ShapeDtypeStruct(rhs.shape, jnp...  31.8 us
    ppermute x7, waiting for transfers between devices, halve(): lax.ppermute(send, 'fh', perm=pairs)  28.1 us
    all_to_all x1, blocking collectives, on_device(): return lax.all_to_all(result, 'fh', split_axis=0, concat_axis=3, tiled=True)  13.1 us
    ppermute x7, starting transfers between devices, halve(): lax.ppermute(send, 'fh', perm=pairs)  12.5 us
    reshape x1, local copies, waits for them, and re-layouts, spectra(): shaped = samples.reshape(antennas_here, symbol_count, 2, FA, FB)  10.9 us
    another operation x1, local copies, waits for them, and re-layouts, spectra(): section_one = jnp.stack([real_part, imag_part], 1).astype(jnp.bfloat16)  9.18 us
    dot_general x1, matrix products, packed_terms(): jnp.einsum('rckm,rclm->rkl', channel, channel, preferred_element_type=jnp...  7.92 us
    concatenate x1, other arithmetic, packed_terms(): return jnp.concatenate([packed, matched_real, matched_imag], 2)  6.88 us
  transfers between devices with their start and end apart: 7, of which 5 were waited for; matrix products, arithmetic and copies ran while one was open for 0% of the time, Pallas kernels for 0%

commit v1 on v0

--- a/solution.py
+++ b/solution.py
@@ -14,7 +14,7 @@
 FA = 16
 FB = 256
 
-PANEL = 8
+PANEL = 16
 PREC = lax.Precision.HIGH
 
 

time: 175 us -> 168 us (0.960)
  Pallas kernels: 31.8 us -> 24.6 us
    pallas_call x1, Pallas kernels: 31.8 us -> 24.6 us  [spd_solve(): pl.pallas_call(_solve_body, out_shape=jax.ShapeDtypeStruct(rhs.shape, jnp...]
where the time goes in v1:
time: 168 us; the launch traced here: 167 us
  matrix products  34.8 us (21%)
  local copies, waits for them, and re-layouts  33.6 us (20%)
  waiting for transfers between devices  28.1 us (17%)
  Pallas kernels  24.6 us (15%)
  other arithmetic  20 us (12%)
  blocking collectives  13.1 us (8%)
  starting transfers between devices  12.5 us (7%)
    ppermute x7, waiting for transfers between devices, halve(): lax.ppermute(send, 'fh', perm=pairs)  28.1 us
    pallas_call x1, Pallas kernels, spd_solve(): pl.pallas_call(_solve_body, out_shape=jax.ShapeDtypeStruct(rhs.shape, jnp...  24.6 us
    all_to_all x1, blocking collectives, on_device(): return lax.all_to_all(result, 'fh', split_axis=0, concat_axis=3, tiled=True)  13.1 us
    ppermute x7, starting transfers between devices, halve(): lax.ppermute(send, 'fh', perm=pairs)  12.5 us
    reshape x1, local copies, waits for them, and re-layouts, spectra(): shaped = samples.reshape(antennas_here, symbol_count, 2, FA, FB)  10.9 us
    another operation x1, local copies, waits for them, and re-layouts, spectra(): section_one = jnp.stack([real_part, imag_part], 1).astype(jnp.bfloat16)  9.18 us
    dot_general x1, matrix products, packed_terms(): jnp.einsum('rckm,rclm->rkl', channel, channel, preferred_element_type=jnp...  7.92 us
    concatenate x1, other arithmetic, packed_terms(): return jnp.concatenate([packed, matched_real, matched_imag], 2)  6.88 us
  transfers between devices with their start and end apart: 7, of which 5 were waited for; matrix products, arithmetic and copies ran while one was open for 0% of the time, Pallas kernels for 0%

profile of v1, /device:TPU:0, one launch (start us, length us, event | category | flops | bytes accessed | tf_op | source)
XLA Modules:
  0.0 167.2 jit_solution(4860279092616738754)
XLA Ops:
  0.0 0.1 negate_convert_fusion.2
  0.1 0.1 fusion.56
  0.1 0.1 sine_multiply_fusion.1
  0.2 1.1 negate_convert_fusion
  1.3 1.0 fusion.33
  2.3 10.9 %reshape.338 = bf16[128,3,2,16,256,1]{4,3,2,1,0,5:T(8,128)(2,1)} reshape(bf16[128,3,2,4096]{3,2,1,0:T(2,128)(2,1)} %param.5) | data formatting | bytes 12582912 | tf_op jit(solution)/shard_map/reshape | solution.py:134
  13.2 4.6 %convolution_bitcast_fusion = f32[3,2,16,256,128]{3,2,0,4,1:T(8,128)S(1)} fusion(bf16[128,3,2,16,256,1]{4,3,2,1,0,5:T(8,128)(2,1)} %reshape.338, bf16[1,16,2,16]{1,3,0,2:T(8,128)(2,1)S(1)} %get-tuple-element.25, bf16[1,16,2,16]{1,3,0,2:T(8,128)(2,1)S(1)} %get-tuple-element.24), kind=kOutput, calls=%fused_computation.8 | convolution fusion | flops 201330688 | bytes 18876416 | tf_op jit(solution)/shard_map/ascnm,cndk->sdkma/dot_general | solution.py:135
  17.8 2.2 %add_convert_fusion = (bf16[3,1,16,256,128]{3,2,0,4,1:T(8,128)(2,1)S(1)}, bf16[3,1,16,256,128]{3,2,0,4,1:T(8,128)(2,1)S(1)}) fusion(f32[3,2,16,256,128]{3,2,0,4,1:T(8,128)S(1)} %convolution_bitcast_fusion, f32[16,256]{1,0:T(8,128)S(1)} %get-tuple-element.31, f32[16,256]{1,0:T(8,128)S(1)} %get-tuple-element.32), kind=kLoop, calls=%fused_computation.7 | loop fusion | flops 12582912 | bytes 18907136 | tf_op jit(solution)/shard_map/convert
  20.0 3.2 %pad_maximum_fusion = bf16[3,2,16,256,128]{3,2,0,4,1:T(8,128)(2,1)} fusion(bf16[3,1,16,256,128]{3,2,0,4,1:T(8,128)(2,1)S(1)} %get-tuple-element.8, bf16[3,1,16,256,128]{3,2,0,4,1:T(8,128)(2,1)S(1)} %get-tuple-element.7), kind=kLoop, calls=%fused_computation.3 | loop fusion | flops 3145728 | bytes 12582912 | tf_op jit(solution)/shard_map/stack | solution.py:143
  23.2 9.2 %copy.99 = bf16[3,2,16,256,128]{4,3,1,2,0:T(8,128)(2,1)} copy(bf16[3,2,16,256,128]{3,2,0,4,1:T(8,128)(2,1)} %pad_maximum_fusion) | data formatting | bytes 12582912 | tf_op jit(solution)/shard_map/stack | solution.py:143
  32.4 6.7 %fusion = bf16[3,2,16,256,128]{4,3,2,0,1:T(8,128)(2,1)S(1)} fusion(bf16[3,2,16,256,128]{4,3,1,2,0:T(8,128)(2,1)} %copy.99, bf16[1,256,2,256]{1,3,0,2:T(8,128)(2,1)S(1)} %get-tuple-element.21, bf16[1,256,2,256]{1,3,0,2:T(8,128)(2,1)S(1)} %get-tuple-element.20), kind=kOutput, calls=%fused_computation.2 | convolution fusion | flops 3225419776 | bytes 13107200 | tf_op jit(solution)/shard_map/sckma,cmdj->sdkja/dot_general | solution.py:144
  39.1 0.3 slice.48
  39.4 2.4 %copy-done.2 = bf16[3,2,16,256,128]{4,3,2,0,1:T(8,128)(2,1)} copy-done((bf16[3,2,16,256,128]{4,3,2,0,1:T(8,128)(2,1)}, bf16[3,2,16,256,128]{4,3,2,0,1:T(8,128)(2,1)S(1)}, u32[]{:S(2)}) %copy-start.2) | copy-done | bytes 6291480
  41.8 0.1 iota_add_fusion
  41.9 0.1 broadcast_add_fusion
  42.0 0.5 copy-done.4
  42.5 0.2 fusion.40
  42.7 5.7 %fusion.4 = bf16[2,64,128,128,1,1,1]{3,1,6,5,2,0,4:T(8,128)(2,1)S(1)} fusion(bf16[2,2,16,128,2,128,1]{5,4,3,2,0,1,6:T(2,128)(2,1)S(1)} %bitcast.136, bf16[1,64,2,2,16,2]{1,4,2,3,0,5:T(8,128)(2,1)S(1)} %get-tuple-element.23, bf16[1,64,2,2,16,2]{1,4,2,3,0,5:T(8,128)(2,1)S(1)} %get-tuple-element.22), kind=kOutput, calls=%fused_computation.13 | convolution fusion | flops 536936448 | bytes 8421376 | tf_op jit(solution)/shard_map/tcarbm,dktcab->rdkm/dot_general | solution.py:215
  48.4 1.0 copy.159
  49.4 0.0 slice-start
  49.4 0.4 slice_negate_fusion
  49.9 1.6 slice-done
  51.4 1.4 copy.105
  52.9 3.2 %convolution_bitcast_fusion.1 = f32[128,64,32]{2,1,0:T(8,128)} fusion(bf16[128,2,32,128]{3,2,0,1:T(8,128)(2,1)S(1)} %bitcast.140, bf16[2,64,128,128,1,1,1]{3,1,6,5,2,0,4:T(8,128)(2,1)S(1)} %fusion.4), kind=kOutput, calls=%fused_computation.18 | convolution fusion | flops 134217728 | bytes 7340032 | tf_op jit(solution)/shard_map/rckm,rcum->rku/dot_general | solution.py:228
  56.1 3.3 %fusion.10 = f32[128,64,32]{2,1,0:T(8,128)} fusion(bf16[128,1,64,128]{3,2,1,0:T(8,128)(2,1)S(1)} %get-tuple-element.10, bf16[128,1,64,128]{3,2,1,0:T(8,128)(2,1)S(1)} %get-tuple-element.9, bf16[128,2,32,128]{3,2,0,1:T(8,128)(2,1)S(1)} %bitcast.141), kind=kOutput, calls=%fused_computation.17 | convolution fusion | flops 136314880 | bytes 7340032 | tf_op jit(solution)/shard_map/rckm,rcum->rku/dot_general | solution.py:229
  59.4 3.4 %fusion.9 = f32[128,64,64,1]{2,1,3,0:T(8,128)} fusion(bf16[128,1,64,128]{3,2,1,0:T(8,128)(2,1)S(1)} %get-tuple-element.10, bf16[128,1,64,128]{3,2,1,0:T(8,128)(2,1)S(1)} %get-tuple-element.9, bf16[2,64,128,128,1,1,1]{3,1,6,5,2,0,4:T(8,128)(2,1)S(1)} %fusion.4), kind=kOutput, calls=%fused_computation.16 | convolution fusion | flops 270532608 | bytes 10485760 | tf_op jit(solution)/shard_map/rckm,rclm->rkl/dot_general | solution.py:220
  62.8 7.9 %bitcast_select_fusion = f32[128,64,64]{2,1,0:T(8,128)} fusion(f32[128,64,64,1]{2,1,3,0:T(8,128)} %fusion.9, pred[64,64]{1,0:T(8,128)(4,1)S(1)} %iota_compare_fusion.3, bf16[2,64,128,128,1,1,1]{3,1,6,5,2,0,4:T(8,128)(2,1)} %copy-done), kind=kOutput, calls=%fused_computation.12 | convolution fusion | flops 268959744 | bytes 8392704 | tf_op jit(solution)/shard_map/rckm,rclm->rkl/dot_general | solution.py:219
  70.7 6.9 %pad_maximum_fusion.2 = f32[128,64,128]{2,1,0:T(8,128)S(1)} fusion(f32[128,64,32]{2,1,0:T(8,128)} %fusion.10, f32[128,64,32]{2,1,0:T(8,128)} %convolution_bitcast_fusion.1, f32[128,64,64]{2,1,0:T(8,128)} %bitcast_select_fusion), kind=kLoop, calls=%fused_computation.11 | loop fusion | flops 2097152 | bytes 8388608 | tf_op jit(solution)/shard_map/concatenate | solution.py:230
  77.6 1.9 %copy-done.1 = f32[128,64,128]{2,1,0:T(8,128)} copy-done((f32[128,64,128]{2,1,0:T(8,128)}, f32[128,64,128]{2,1,0:T(8,128)S(1)}, u32[]{:S(2)}) %copy-start.1) | copy-done | bytes 4194328
  79.6 1.5 dynamic-slice_bitcast_fusion
  81.1 0.4 collective-permute-start
  81.5 4.0 %collective-permute-done = f32[2,2,2,8,64,128]{5,4,3,2,1,0:T(8,128)S(1)} collective-permute-done((f32[2,2,2,8,64,128]{5,4,3,2,1,0:T(8,128)}, f32[2,2,2,8,64,128]{5,4,3,2,1,0:T(8,128)S(1)}, u32[]{:S(2)}, u32[]{:S(2)}) %collective-permute-start) | collective-permute-done | bytes 2097184 | tf_op jit(solution)/shard_map/ppermute | solution.py:254
  85.5 2.0 %bitcast_add_fusion = f32[2,2,2,8,64,128]{5,4,3,2,1,0:T(8,128)S(1)} fusion(f32[2,2,2,8,64,128]{5,4,3,2,1,0:T(8,128)S(1)} %collective-permute-done, f32[2,2,2,2,8,64,128]{6,5,4,3,2,1,0:T(8,128)} %bitcast.139, s32[]{:T(128)S(6)} %select_n.150), kind=kLoop, calls=%fused_computation.20 | loop fusion | flops 524288 | bytes 6291460 | tf_op jit(solution)/shard_map/add | solution.py:254
  87.5 0.0 copy-start.5
  87.5 0.0 copy-start.6
  87.5 0.2 fusion.64
  87.7 0.0 copy-start.3
  87.7 0.1 constant_dynamic-slice_fusion.3
  87.9 3.0 %collective-permute-start.1 = (f32[2,2,4,64,128]{4,3,2,0,1:T(8,128)S(1)}, f32[2,2,4,64,128]{4,3,2,0,1:T(8,128)S(1)}, u32[]{:S(2)}, u32[]{:S(2)}) collective-permute-start(f32[2,2,4,64,128]{4,3,2,0,1:T(8,128)S(1)} %bitcast.145), channel_id=1, source_target_pairs={{0,2},{1,3},{2,0},{3,1},{4,6},{5,7},{6,4},{7,5},{8,10},{9,11},{10,... | collective-permute-start | bytes 1572872 | tf_op jit(solution)/shard_map/ppermute | solution.py:254
  90.9 0.1 constant_dynamic-slice_fusion.1
  91.0 1.7 %collective-permute-start.4 = (f32[2,2,4,64,128]{4,3,2,0,1:T(8,128)S(1)}, f32[2,2,4,64,128]{4,3,2,0,1:T(8,128)S(1)}, u32[]{:S(2)}, u32[]{:S(2)}) collective-permute-start(f32[2,2,4,64,128]{4,3,2,0,1:T(8,128)S(1)} %bitcast.146), channel_id=1, source_target_pairs={{0,4},{1,5},{2,6},{3,7},{4,0},{5,1},{6,2},{7,3},{8,12},{9,13},{10,... | collective-permute-start | bytes 1572872 | tf_op jit(solution)/shard_map/ppermute | solution.py:254
  92.7 10.3 %collective-permute-done.1 = f32[2,2,4,64,128]{4,3,2,0,1:T(8,128)S(1)} collective-permute-done((f32[2,2,4,64,128]{4,3,2,0,1:T(8,128)S(1)}, f32[2,2,4,64,128]{4,3,2,0,1:T(8,128)S(1)}, u32[]{:S(2)}, u32[]{:S(2)}) %collective-permute-start.1) | collective-permute-done | bytes 524320 | tf_op jit(solution)/shard_map/ppermute | solution.py:254
  103.0 0.1 bitcast_add_fusion.2
  103.1 1.9 %collective-permute-start.2 = (f32[2,4,64,128]{3,2,1,0:T(8,128)S(1)}, f32[2,4,64,128]{3,2,1,0:T(8,128)S(1)}, u32[]{:S(2)}, u32[]{:S(2)}) collective-permute-start(f32[2,4,64,128]{3,2,1,0:T(8,128)S(1)} %dynamic-slice_bitcast_fusion.2), channel_id=1, source_target_pairs={{0,4},{1,5},{2,6},{3,7},{4,0},{5,1},{6,2},{7,3},{8,12},{9,13},{10,... | collective-permute-start | bytes 786440 | tf_op jit(solution)/shard_map/ppermute | solution.py:254
  105.0 0.0 collective-permute-done.4
  105.0 0.1 bitcast_add_fusion.1
  105.1 1.6 collective-permute-start.5
  106.7 4.3 %collective-permute-done.2 = f32[2,4,64,128]{3,2,1,0:T(8,128)S(1)} collective-permute-done((f32[2,4,64,128]{3,2,1,0:T(8,128)S(1)}, f32[2,4,64,128]{3,2,1,0:T(8,128)S(1)}, u32[]{:S(2)}, u32[]{:S(2)}) %collective-permute-start.2) | collective-permute-done | bytes 262176 | tf_op jit(solution)/shard_map/ppermute | solution.py:254
  111.1 2.6 %collective-permute-start.3 = (f32[4,64,128]{2,1,0:T(8,128)S(1)}, f32[4,64,128]{2,1,0:T(8,128)S(1)}, u32[]{:S(2)}, u32[]{:S(2)}) collective-permute-start(f32[4,64,128]{2,1,0:T(8,128)S(1)} %dynamic-slice_bitcast_fusion.4), channel_id=1, source_target_pairs={{0,8},{1,9},{2,10},{3,11},{4,12},{5,13},{6,14},{7,15},{8,0},{9,1},... | collective-permute-start | bytes 393224 | tf_op jit(solution)/shard_map/ppermute | solution.py:254
  113.7 0.0 collective-permute-done.5
  113.7 1.4 collective-permute-start.6
  115.1 7.6 %collective-permute-done.3 = f32[4,64,128]{2,1,0:T(8,128)S(1)} collective-permute-done((f32[4,64,128]{2,1,0:T(8,128)S(1)}, f32[4,64,128]{2,1,0:T(8,128)S(1)}, u32[]{:S(2)}, u32[]{:S(2)}) %collective-permute-start.3) | collective-permute-done | bytes 131104 | tf_op jit(solution)/shard_map/ppermute | solution.py:254
  122.7 1.9 %collective-permute-done.6 = f32[4,64,128]{2,1,0:T(8,128)S(1)} collective-permute-done((f32[4,64,128]{2,1,0:T(8,128)S(1)}, f32[4,64,128]{2,1,0:T(8,128)S(1)}, u32[]{:S(2)}, u32[]{:S(2)}) %collective-permute-start.6) | collective-permute-done | bytes 131104 | tf_op jit(solution)/shard_map/ppermute | solution.py:254
  124.7 0.1 copy.114
  124.8 0.3 fusion.17
  125.1 0.8 pad_maximum_fusion.7.b_ref
  125.9 0.2 fusion.62
  126.1 1.0 maximum_maximum_fusion.a_ref
  127.2 24.6 %shard_map.55 = f32[8,128,32]{2,1,0:T(8,128)} custom-call(f32[8,128,128]{2,1,0:T(8,128)} %maximum_maximum_fusion.a_ref, f32[8,128,32]{2,1,0:T(8,128)} %pad_maximum_fusion.7.b_ref), custom_call_target="tpu_custom_call" | custom-call | tf_op jit(solution)/shard_map/pallas_call | solution.py:100
  151.8 1.2 copy.115
  153.0 0.2 reshape.335
  153.2 0.1 copy.117
  153.4 13.1 %all_to_all.18 = f32[64,1,2,256]{3,2,1,0:T(2,128)S(1)} all-to-all(f32[64,1,2,256]{3,2,1,0:T(2,128)S(1)} %copy.117), channel_id=1, replica_groups=mesh['cells'=2,'fh'=16] {'fh'}, dimensions={0} | all-to-all | bytes 262144 | tf_op jit(solution)/shard_map/all_to_all | solution.py:288
  166.5 0.7 copy.142
  (30 shorter events, 0.4 us)
Async XLA Ops:
  39.1 2.7 %copy-start.2 = (bf16[3,2,16,256,128]{4,3,2,0,1:T(8,128)(2,1)}, bf16[3,2,16,256,128]{4,3,2,0,1:T(8,128)(2,1)S(1)}, u32[]{:S(2)}) copy-start(bf16[3,2,16,256,128]{4,3,2,0,1:T(8,128)(2,1)S(1)} %fusion) | copy-start | bytes 18874372
  41.8 0.7 copy-start.4
  48.4 11.0 %copy-start = (bf16[2,64,128,128,1,1,1]{3,1,6,5,2,0,4:T(8,128)(2,1)}, bf16[2,64,128,128,1,1,1]{3,1,6,5,2,0,4:T(8,128)(2,1)S(1)}, u32[]{:S(2)}) copy-start(bf16[2,64,128,128,1,1,1]{3,1,6,5,2,0,4:T(8,128)(2,1)S(1)} %fusion.4) | copy-start | bytes 12582916
  49.4 2.0 %slice-start = ((bf16[3,2,16,256,128]{4,3,2,0,1:T(8,128)(2,1)}), bf16[1,2,16,256,128]{4,3,2,0,1:T(8,128)(2,1)S(1)}, s32[]{:S(2)}) async-start(bf16[3,2,16,256,128]{4,3,2,0,1:T(8,128)(2,1)} %copy-done.2), calls=%async_computation.1 | async-start | bytes 4194304 | tf_op jit(solution)/shard_map/slice | solution.py:282
  77.6 2.0 %copy-start.1 = (f32[128,64,128]{2,1,0:T(8,128)}, f32[128,64,128]{2,1,0:T(8,128)S(1)}, u32[]{:S(2)}) copy-start(f32[128,64,128]{2,1,0:T(8,128)S(1)} %pad_maximum_fusion.2) | copy-start | bytes 12582916
  81.1 4.4 %collective-permute-start = (f32[2,2,2,8,64,128]{5,4,3,2,1,0:T(8,128)}, f32[2,2,2,8,64,128]{5,4,3,2,1,0:T(8,128)S(1)}, u32[]{:S(2)}, u32[]{:S(2)}) collective-permute-start(f32[2,2,2,8,64,128]{5,4,3,2,1,0:T(8,128)} %dynamic-slice_bitcast_fusion), channel_id=1, source_target_pairs={{0,1},{1,0},{2,3},{3,2},{4,5},{5,4},{6,7},{7,6},{8,9},{9,8},{10,11... | collective-permute-start | bytes 6291464 | tf_op jit(solution)/shard_map/ppermute | solution.py:254
  87.5 3.3 %copy-start.5 = (f32[64]{0:T(128)S(1)}, f32[64]{0:T(128)}, u32[]{:S(2)}) copy-start(f32[64]{0:T(128)} %param.9) | copy-start | bytes 772
  87.5 3.3 %copy-start.6 = (s32[64]{0:T(128)S(1)}, s32[64]{0:T(128)}, u32[]{:S(2)}) copy-start(s32[64]{0:T(128)} %param.7) | copy-start | bytes 772
  87.7 5.0 %copy-start.3 = (s32[8,64]{1,0:T(8,128)S(1)}, s32[8,64]{1,0:T(8,128)}, u32[]{:S(2)}) copy-start(s32[8,64]{1,0:T(8,128)} %param.8) | copy-start | bytes 6148
  87.9 15.2 %collective-permute-start.1 = (f32[2,2,4,64,128]{4,3,2,0,1:T(8,128)S(1)}, f32[2,2,4,64,128]{4,3,2,0,1:T(8,128)S(1)}, u32[]{:S(2)}, u32[]{:S(2)}) collective-permute-start(f32[2,2,4,64,128]{4,3,2,0,1:T(8,128)S(1)} %bitcast.145), channel_id=1, source_target_pairs={{0,2},{1,3},{2,0},{3,1},{4,6},{5,7},{6,4},{7,5},{8,10},{9,11},{10,... | collective-permute-start | bytes 1572872 | tf_op jit(solution)/shard_map/ppermute | solution.py:254
  91.0 14.0 %collective-permute-start.4 = (f32[2,2,4,64,128]{4,3,2,0,1:T(8,128)S(1)}, f32[2,2,4,64,128]{4,3,2,0,1:T(8,128)S(1)}, u32[]{:S(2)}, u32[]{:S(2)}) collective-permute-start(f32[2,2,4,64,128]{4,3,2,0,1:T(8,128)S(1)} %bitcast.146), channel_id=1, source_target_pairs={{0,4},{1,5},{2,6},{3,7},{4,0},{5,1},{6,2},{7,3},{8,12},{9,13},{10,... | collective-permute-start | bytes 1572872 | tf_op jit(solution)/shard_map/ppermute | solution.py:254
  103.1 7.9 %collective-permute-start.2 = (f32[2,4,64,128]{3,2,1,0:T(8,128)S(1)}, f32[2,4,64,128]{3,2,1,0:T(8,128)S(1)}, u32[]{:S(2)}, u32[]{:S(2)}) collective-permute-start(f32[2,4,64,128]{3,2,1,0:T(8,128)S(1)} %dynamic-slice_bitcast_fusion.2), channel_id=1, source_target_pairs={{0,4},{1,5},{2,6},{3,7},{4,0},{5,1},{6,2},{7,3},{8,12},{9,13},{10,... | collective-permute-start | bytes 786440 | tf_op jit(solution)/shard_map/ppermute | solution.py:254
  105.1 8.6 %collective-permute-start.5 = (f32[2,4,64,128]{3,2,1,0:T(8,128)S(1)}, f32[2,4,64,128]{3,2,1,0:T(8,128)S(1)}, u32[]{:S(2)}, u32[]{:S(2)}) collective-permute-start(f32[2,4,64,128]{3,2,1,0:T(8,128)S(1)} %dynamic-slice_bitcast_fusion.1), channel_id=1, source_target_pairs={{0,2},{1,3},{2,0},{3,1},{4,6},{5,7},{6,4},{7,5},{8,10},{9,11},{10,... | collective-permute-start | bytes 786440 | tf_op jit(solution)/shard_map/ppermute | solution.py:254
  111.1 11.6 %collective-permute-start.3 = (f32[4,64,128]{2,1,0:T(8,128)S(1)}, f32[4,64,128]{2,1,0:T(8,128)S(1)}, u32[]{:S(2)}, u32[]{:S(2)}) collective-permute-start(f32[4,64,128]{2,1,0:T(8,128)S(1)} %dynamic-slice_bitcast_fusion.4), channel_id=1, source_target_pairs={{0,8},{1,9},{2,10},{3,11},{4,12},{5,13},{6,14},{7,15},{8,0},{9,1},... | collective-permute-start | bytes 393224 | tf_op jit(solution)/shard_map/ppermute | solution.py:254
  113.7 10.9 %collective-permute-start.6 = (f32[4,64,128]{2,1,0:T(8,128)S(1)}, f32[4,64,128]{2,1,0:T(8,128)S(1)}, u32[]{:S(2)}, u32[]{:S(2)}) collective-permute-start(f32[4,64,128]{2,1,0:T(8,128)S(1)} %dynamic-slice_bitcast_fusion.3), channel_id=1, source_target_pairs={{0,8},{1,9},{2,10},{3,11},{4,12},{5,13},{6,14},{7,15},{8,0},{9,1},... | collective-permute-start | bytes 393224 | tf_op jit(solution)/shard_map/ppermute | solution.py:254

commit v2 on v1

--- a/solution.py
+++ b/solution.py
@@ -14,7 +14,7 @@
 FA = 16
 FB = 256
 
-PANEL = 16
+PANEL = 32
 PREC = lax.Precision.HIGH
 
 
@@ -62,7 +62,7 @@
             r_ref[b] = r_ref[b] - update[:, n:]
         return carry
 
-    looped = panels // 2
+    looped = panels - 1
     lax.fori_loop(0, looped, functools.partial(forward, fixed=False), 0)
     for p in range(looped, panels):
         forward(p, 0)

time: 168 us -> 165 us (0.982)
  Pallas kernels: 24.6 us -> 22.1 us
    pallas_call x1, Pallas kernels: 24.6 us -> 22.1 us  [spd_solve(): pl.pallas_call(_solve_body, out_shape=jax.ShapeDtypeStruct(rhs.shape, jnp...]
where the time goes in v2:
time: 165 us
  matrix products  34.8 us (21%)
  local copies, waits for them, and re-layouts  33.6 us (20%)
  waiting for transfers between devices  28.1 us (17%)
  Pallas kernels  22.1 us (13%)
  other arithmetic  20 us (12%)
  blocking collectives  13.1 us (8%)
  starting transfers between devices  12.5 us (8%)
    ppermute x7, waiting for transfers between devices, halve(): lax.ppermute(send, 'fh', perm=pairs)  28.1 us
    pallas_call x1, Pallas kernels, spd_solve(): pl.pallas_call(_solve_body, out_shape=jax.ShapeDtypeStruct(rhs.shape, jnp...  22.1 us
    all_to_all x1, blocking collectives, on_device(): return lax.all_to_all(result, 'fh', split_axis=0, concat_axis=3, tiled=True)  13.1 us
    ppermute x7, starting transfers between devices, halve(): lax.ppermute(send, 'fh', perm=pairs)  12.5 us
    reshape x1, local copies, waits for them, and re-layouts, spectra(): shaped = samples.reshape(antennas_here, symbol_count, 2, FA, FB)  10.9 us
    another operation x1, local copies, waits for them, and re-layouts, spectra(): section_one = jnp.stack([real_part, imag_part], 1).astype(jnp.bfloat16)  9.18 us
    dot_general x1, matrix products, packed_terms(): jnp.einsum('rckm,rclm->rkl', channel, channel, preferred_element_type=jnp...  7.92 us
    concatenate x1, other arithmetic, packed_terms(): return jnp.concatenate([packed, matched_real, matched_imag], 2)  6.88 us
  transfers between devices with their start and end apart: 7, of which 5 were waited for; matrix products, arithmetic and copies ran while one was open for 0% of the time, Pallas kernels for 0%

profile of v2, /device:TPU:0, one launch (start us, length us, event | category | flops | bytes accessed | tf_op | source)
XLA Modules:
  0.0 164.7 jit_solution(14463467491438185433)
XLA Ops:
  0.0 0.1 negate_convert_fusion.2
  0.1 0.1 fusion.56
  0.1 0.1 sine_multiply_fusion.1
  0.2 1.1 negate_convert_fusion
  1.3 1.0 fusion.33
  2.3 10.9 %reshape.338 = bf16[128,3,2,16,256,1]{4,3,2,1,0,5:T(8,128)(2,1)} reshape(bf16[128,3,2,4096]{3,2,1,0:T(2,128)(2,1)} %param.5) | data formatting | bytes 12582912 | tf_op jit(solution)/shard_map/reshape | solution.py:134
  13.2 4.6 %convolution_bitcast_fusion = f32[3,2,16,256,128]{3,2,0,4,1:T(8,128)S(1)} fusion(bf16[128,3,2,16,256,1]{4,3,2,1,0,5:T(8,128)(2,1)} %reshape.338, bf16[1,16,2,16]{1,3,0,2:T(8,128)(2,1)S(1)} %get-tuple-element.25, bf16[1,16,2,16]{1,3,0,2:T(8,128)(2,1)S(1)} %get-tuple-element.24), kind=kOutput, calls=%fused_computation.8 | convolution fusion | flops 201330688 | bytes 18876416 | tf_op jit(solution)/shard_map/ascnm,cndk->sdkma/dot_general | solution.py:135
  17.8 2.2 %add_convert_fusion = (bf16[3,1,16,256,128]{3,2,0,4,1:T(8,128)(2,1)S(1)}, bf16[3,1,16,256,128]{3,2,0,4,1:T(8,128)(2,1)S(1)}) fusion(f32[3,2,16,256,128]{3,2,0,4,1:T(8,128)S(1)} %convolution_bitcast_fusion, f32[16,256]{1,0:T(8,128)S(1)} %get-tuple-element.31, f32[16,256]{1,0:T(8,128)S(1)} %get-tuple-element.32), kind=kLoop, calls=%fused_computation.7 | loop fusion | flops 12582912 | bytes 18907136 | tf_op jit(solution)/shard_map/convert
  20.0 3.2 %pad_maximum_fusion = bf16[3,2,16,256,128]{3,2,0,4,1:T(8,128)(2,1)} fusion(bf16[3,1,16,256,128]{3,2,0,4,1:T(8,128)(2,1)S(1)} %get-tuple-element.8, bf16[3,1,16,256,128]{3,2,0,4,1:T(8,128)(2,1)S(1)} %get-tuple-element.7), kind=kLoop, calls=%fused_computation.3 | loop fusion | flops 3145728 | bytes 12582912 | tf_op jit(solution)/shard_map/stack | solution.py:143
  23.2 9.2 %copy.99 = bf16[3,2,16,256,128]{4,3,1,2,0:T(8,128)(2,1)} copy(bf16[3,2,16,256,128]{3,2,0,4,1:T(8,128)(2,1)} %pad_maximum_fusion) | data formatting | bytes 12582912 | tf_op jit(solution)/shard_map/stack | solution.py:143
  32.4 6.7 %fusion = bf16[3,2,16,256,128]{4,3,2,0,1:T(8,128)(2,1)S(1)} fusion(bf16[3,2,16,256,128]{4,3,1,2,0:T(8,128)(2,1)} %copy.99, bf16[1,256,2,256]{1,3,0,2:T(8,128)(2,1)S(1)} %get-tuple-element.21, bf16[1,256,2,256]{1,3,0,2:T(8,128)(2,1)S(1)} %get-tuple-element.20), kind=kOutput, calls=%fused_computation.2 | convolution fusion | flops 3225419776 | bytes 13107200 | tf_op jit(solution)/shard_map/sckma,cmdj->sdkja/dot_general | solution.py:144
  39.1 0.3 slice.48
  39.4 2.4 %copy-done.2 = bf16[3,2,16,256,128]{4,3,2,0,1:T(8,128)(2,1)} copy-done((bf16[3,2,16,256,128]{4,3,2,0,1:T(8,128)(2,1)}, bf16[3,2,16,256,128]{4,3,2,0,1:T(8,128)(2,1)S(1)}, u32[]{:S(2)}) %copy-start.2) | copy-done | bytes 6291480
  41.8 0.1 iota_add_fusion
  41.9 0.1 broadcast_add_fusion
  42.0 0.5 copy-done.4
  42.5 0.2 fusion.40
  42.7 5.7 %fusion.4 = bf16[2,64,128,128,1,1,1]{3,1,6,5,2,0,4:T(8,128)(2,1)S(1)} fusion(bf16[2,2,16,128,2,128,1]{5,4,3,2,0,1,6:T(2,128)(2,1)S(1)} %bitcast.136, bf16[1,64,2,2,16,2]{1,4,2,3,0,5:T(8,128)(2,1)S(1)} %get-tuple-element.23, bf16[1,64,2,2,16,2]{1,4,2,3,0,5:T(8,128)(2,1)S(1)} %get-tuple-element.22), kind=kOutput, calls=%fused_computation.13 | convolution fusion | flops 536936448 | bytes 8421376 | tf_op jit(solution)/shard_map/tcarbm,dktcab->rdkm/dot_general | solution.py:215
  48.4 1.0 copy.159
  49.4 0.0 slice-start
  49.4 0.4 slice_negate_fusion
  49.9 1.6 slice-done
  51.4 1.4 copy.105
  52.9 3.2 %convolution_bitcast_fusion.1 = f32[128,64,32]{2,1,0:T(8,128)} fusion(bf16[128,2,32,128]{3,2,0,1:T(8,128)(2,1)S(1)} %bitcast.140, bf16[2,64,128,128,1,1,1]{3,1,6,5,2,0,4:T(8,128)(2,1)S(1)} %fusion.4), kind=kOutput, calls=%fused_computation.18 | convolution fusion | flops 134217728 | bytes 7340032 | tf_op jit(solution)/shard_map/rckm,rcum->rku/dot_general | solution.py:228
  56.1 3.3 %fusion.10 = f32[128,64,32]{2,1,0:T(8,128)} fusion(bf16[128,1,64,128]{3,2,1,0:T(8,128)(2,1)S(1)} %get-tuple-element.10, bf16[128,1,64,128]{3,2,1,0:T(8,128)(2,1)S(1)} %get-tuple-element.9, bf16[128,2,32,128]{3,2,0,1:T(8,128)(2,1)S(1)} %bitcast.141), kind=kOutput, calls=%fused_computation.17 | convolution fusion | flops 136314880 | bytes 7340032 | tf_op jit(solution)/shard_map/rckm,rcum->rku/dot_general | solution.py:229
  59.4 3.4 %fusion.9 = f32[128,64,64,1]{2,1,3,0:T(8,128)} fusion(bf16[128,1,64,128]{3,2,1,0:T(8,128)(2,1)S(1)} %get-tuple-element.10, bf16[128,1,64,128]{3,2,1,0:T(8,128)(2,1)S(1)} %get-tuple-element.9, bf16[2,64,128,128,1,1,1]{3,1,6,5,2,0,4:T(8,128)(2,1)S(1)} %fusion.4), kind=kOutput, calls=%fused_computation.16 | convolution fusion | flops 270532608 | bytes 10485760 | tf_op jit(solution)/shard_map/rckm,rclm->rkl/dot_general | solution.py:220
  62.8 7.9 %bitcast_select_fusion = f32[128,64,64]{2,1,0:T(8,128)} fusion(f32[128,64,64,1]{2,1,3,0:T(8,128)} %fusion.9, pred[64,64]{1,0:T(8,128)(4,1)S(1)} %iota_compare_fusion.3, bf16[2,64,128,128,1,1,1]{3,1,6,5,2,0,4:T(8,128)(2,1)} %copy-done), kind=kOutput, calls=%fused_computation.12 | convolution fusion | flops 268959744 | bytes 8392704 | tf_op jit(solution)/shard_map/rckm,rclm->rkl/dot_general | solution.py:219
  70.7 6.9 %pad_maximum_fusion.2 = f32[128,64,128]{2,1,0:T(8,128)S(1)} fusion(f32[128,64,32]{2,1,0:T(8,128)} %fusion.10, f32[128,64,32]{2,1,0:T(8,128)} %convolution_bitcast_fusion.1, f32[128,64,64]{2,1,0:T(8,128)} %bitcast_select_fusion), kind=kLoop, calls=%fused_computation.11 | loop fusion | flops 2097152 | bytes 8388608 | tf_op jit(solution)/shard_map/concatenate | solution.py:230
  77.6 1.9 %copy-done.1 = f32[128,64,128]{2,1,0:T(8,128)} copy-done((f32[128,64,128]{2,1,0:T(8,128)}, f32[128,64,128]{2,1,0:T(8,128)S(1)}, u32[]{:S(2)}) %copy-start.1) | copy-done | bytes 4194328
  79.6 1.5 dynamic-slice_bitcast_fusion
  81.1 0.4 collective-permute-start
  81.5 4.0 %collective-permute-done = f32[2,2,2,8,64,128]{5,4,3,2,1,0:T(8,128)S(1)} collective-permute-done((f32[2,2,2,8,64,128]{5,4,3,2,1,0:T(8,128)}, f32[2,2,2,8,64,128]{5,4,3,2,1,0:T(8,128)S(1)}, u32[]{:S(2)}, u32[]{:S(2)}) %collective-permute-start) | collective-permute-done | bytes 2097184 | tf_op jit(solution)/shard_map/ppermute | solution.py:254
  85.5 2.0 %bitcast_add_fusion = f32[2,2,2,8,64,128]{5,4,3,2,1,0:T(8,128)S(1)} fusion(f32[2,2,2,8,64,128]{5,4,3,2,1,0:T(8,128)S(1)} %collective-permute-done, f32[2,2,2,2,8,64,128]{6,5,4,3,2,1,0:T(8,128)} %bitcast.139, s32[]{:T(128)S(6)} %select_n.150), kind=kLoop, calls=%fused_computation.20 | loop fusion | flops 524288 | bytes 6291460 | tf_op jit(solution)/shard_map/add | solution.py:254
  87.5 0.0 copy-start.5
  87.5 0.0 copy-start.6
  87.5 0.2 fusion.64
  87.7 0.0 copy-start.3
  87.7 0.1 constant_dynamic-slice_fusion.3
  87.9 3.0 %collective-permute-start.1 = (f32[2,2,4,64,128]{4,3,2,0,1:T(8,128)S(1)}, f32[2,2,4,64,128]{4,3,2,0,1:T(8,128)S(1)}, u32[]{:S(2)}, u32[]{:S(2)}) collective-permute-start(f32[2,2,4,64,128]{4,3,2,0,1:T(8,128)S(1)} %bitcast.145), channel_id=1, source_target_pairs={{0,2},{1,3},{2,0},{3,1},{4,6},{5,7},{6,4},{7,5},{8,10},{9,11},{10,... | collective-permute-start | bytes 1572872 | tf_op jit(solution)/shard_map/ppermute | solution.py:254
  90.9 0.1 constant_dynamic-slice_fusion.1
  91.0 1.7 %collective-permute-start.4 = (f32[2,2,4,64,128]{4,3,2,0,1:T(8,128)S(1)}, f32[2,2,4,64,128]{4,3,2,0,1:T(8,128)S(1)}, u32[]{:S(2)}, u32[]{:S(2)}) collective-permute-start(f32[2,2,4,64,128]{4,3,2,0,1:T(8,128)S(1)} %bitcast.146), channel_id=1, source_target_pairs={{0,4},{1,5},{2,6},{3,7},{4,0},{5,1},{6,2},{7,3},{8,12},{9,13},{10,... | collective-permute-start | bytes 1572872 | tf_op jit(solution)/shard_map/ppermute | solution.py:254
  92.7 10.3 %collective-permute-done.1 = f32[2,2,4,64,128]{4,3,2,0,1:T(8,128)S(1)} collective-permute-done((f32[2,2,4,64,128]{4,3,2,0,1:T(8,128)S(1)}, f32[2,2,4,64,128]{4,3,2,0,1:T(8,128)S(1)}, u32[]{:S(2)}, u32[]{:S(2)}) %collective-permute-start.1) | collective-permute-done | bytes 524320 | tf_op jit(solution)/shard_map/ppermute | solution.py:254
  103.0 0.1 bitcast_add_fusion.2
  103.1 1.9 %collective-permute-start.2 = (f32[2,4,64,128]{3,2,1,0:T(8,128)S(1)}, f32[2,4,64,128]{3,2,1,0:T(8,128)S(1)}, u32[]{:S(2)}, u32[]{:S(2)}) collective-permute-start(f32[2,4,64,128]{3,2,1,0:T(8,128)S(1)} %dynamic-slice_bitcast_fusion.2), channel_id=1, source_target_pairs={{0,4},{1,5},{2,6},{3,7},{4,0},{5,1},{6,2},{7,3},{8,12},{9,13},{10,... | collective-permute-start | bytes 786440 | tf_op jit(solution)/shard_map/ppermute | solution.py:254
  105.0 0.0 collective-permute-done.4
  105.0 0.1 bitcast_add_fusion.1
  105.1 1.6 collective-permute-start.5
  106.7 4.3 %collective-permute-done.2 = f32[2,4,64,128]{3,2,1,0:T(8,128)S(1)} collective-permute-done((f32[2,4,64,128]{3,2,1,0:T(8,128)S(1)}, f32[2,4,64,128]{3,2,1,0:T(8,128)S(1)}, u32[]{:S(2)}, u32[]{:S(2)}) %collective-permute-start.2) | collective-permute-done | bytes 262176 | tf_op jit(solution)/shard_map/ppermute | solution.py:254
  111.1 2.6 %collective-permute-start.3 = (f32[4,64,128]{2,1,0:T(8,128)S(1)}, f32[4,64,128]{2,1,0:T(8,128)S(1)}, u32[]{:S(2)}, u32[]{:S(2)}) collective-permute-start(f32[4,64,128]{2,1,0:T(8,128)S(1)} %dynamic-slice_bitcast_fusion.4), channel_id=1, source_target_pairs={{0,8},{1,9},{2,10},{3,11},{4,12},{5,13},{6,14},{7,15},{8,0},{9,1},... | collective-permute-start | bytes 393224 | tf_op jit(solution)/shard_map/ppermute | solution.py:254
  113.7 0.0 collective-permute-done.5
  113.7 1.4 collective-permute-start.6
  115.1 7.6 %collective-permute-done.3 = f32[4,64,128]{2,1,0:T(8,128)S(1)} collective-permute-done((f32[4,64,128]{2,1,0:T(8,128)S(1)}, f32[4,64,128]{2,1,0:T(8,128)S(1)}, u32[]{:S(2)}, u32[]{:S(2)}) %collective-permute-start.3) | collective-permute-done | bytes 131104 | tf_op jit(solution)/shard_map/ppermute | solution.py:254
  122.7 1.9 %collective-permute-done.6 = f32[4,64,128]{2,1,0:T(8,128)S(1)} collective-permute-done((f32[4,64,128]{2,1,0:T(8,128)S(1)}, f32[4,64,128]{2,1,0:T(8,128)S(1)}, u32[]{:S(2)}, u32[]{:S(2)}) %collective-permute-start.6) | collective-permute-done | bytes 131104 | tf_op jit(solution)/shard_map/ppermute | solution.py:254
  124.7 0.1 copy.114
  124.8 0.3 fusion.17
  125.1 0.8 pad_maximum_fusion.7.b_ref
  125.9 0.2 fusion.62
  126.1 1.0 maximum_maximum_fusion.a_ref
  127.2 22.1 %shard_map.55 = f32[8,128,32]{2,1,0:T(8,128)} custom-call(f32[8,128,128]{2,1,0:T(8,128)} %maximum_maximum_fusion.a_ref, f32[8,128,32]{2,1,0:T(8,128)} %pad_maximum_fusion.7.b_ref), custom_call_target="tpu_custom_call" | custom-call | tf_op jit(solution)/shard_map/pallas_call | solution.py:100
  149.3 1.2 copy.115
  150.5 0.2 reshape.335
  150.7 0.1 copy.117
  150.8 13.1 %all_to_all.18 = f32[64,1,2,256]{3,2,1,0:T(2,128)S(1)} all-to-all(f32[64,1,2,256]{3,2,1,0:T(2,128)S(1)} %copy.117), channel_id=1, replica_groups=mesh['cells'=2,'fh'=16] {'fh'}, dimensions={0} | all-to-all | bytes 262144 | tf_op jit(solution)/shard_map/all_to_all | solution.py:288
  164.0 0.7 copy.142
  (30 shorter events, 0.4 us)
Async XLA Ops:
  39.1 2.7 %copy-start.2 = (bf16[3,2,16,256,128]{4,3,2,0,1:T(8,128)(2,1)}, bf16[3,2,16,256,128]{4,3,2,0,1:T(8,128)(2,1)S(1)}, u32[]{:S(2)}) copy-start(bf16[3,2,16,256,128]{4,3,2,0,1:T(8,128)(2,1)S(1)} %fusion) | copy-start | bytes 18874372
  41.8 0.7 copy-start.4
  48.4 11.0 %copy-start = (bf16[2,64,128,128,1,1,1]{3,1,6,5,2,0,4:T(8,128)(2,1)}, bf16[2,64,128,128,1,1,1]{3,1,6,5,2,0,4:T(8,128)(2,1)S(1)}, u32[]{:S(2)}) copy-start(bf16[2,64,128,128,1,1,1]{3,1,6,5,2,0,4:T(8,128)(2,1)S(1)} %fusion.4) | copy-start | bytes 12582916
  49.4 2.0 %slice-start = ((bf16[3,2,16,256,128]{4,3,2,0,1:T(8,128)(2,1)}), bf16[1,2,16,256,128]{4,3,2,0,1:T(8,128)(2,1)S(1)}, s32[]{:S(2)}) async-start(bf16[3,2,16,256,128]{4,3,2,0,1:T(8,128)(2,1)} %copy-done.2), calls=%async_computation.1 | async-start | bytes 4194304 | tf_op jit(solution)/shard_map/slice | solution.py:282
  77.6 2.0 %copy-start.1 = (f32[128,64,128]{2,1,0:T(8,128)}, f32[128,64,128]{2,1,0:T(8,128)S(1)}, u32[]{:S(2)}) copy-start(f32[128,64,128]{2,1,0:T(8,128)S(1)} %pad_maximum_fusion.2) | copy-start | bytes 12582916
  81.1 4.4 %collective-permute-start = (f32[2,2,2,8,64,128]{5,4,3,2,1,0:T(8,128)}, f32[2,2,2,8,64,128]{5,4,3,2,1,0:T(8,128)S(1)}, u32[]{:S(2)}, u32[]{:S(2)}) collective-permute-start(f32[2,2,2,8,64,128]{5,4,3,2,1,0:T(8,128)} %dynamic-slice_bitcast_fusion), channel_id=1, source_target_pairs={{0,1},{1,0},{2,3},{3,2},{4,5},{5,4},{6,7},{7,6},{8,9},{9,8},{10,11... | collective-permute-start | bytes 6291464 | tf_op jit(solution)/shard_map/ppermute | solution.py:254
  87.5 3.3 %copy-start.5 = (f32[64]{0:T(128)S(1)}, f32[64]{0:T(128)}, u32[]{:S(2)}) copy-start(f32[64]{0:T(128)} %param.9) | copy-start | bytes 772
  87.5 3.3 %copy-start.6 = (s32[64]{0:T(128)S(1)}, s32[64]{0:T(128)}, u32[]{:S(2)}) copy-start(s32[64]{0:T(128)} %param.7) | copy-start | bytes 772
  87.7 5.0 %copy-start.3 = (s32[8,64]{1,0:T(8,128)S(1)}, s32[8,64]{1,0:T(8,128)}, u32[]{:S(2)}) copy-start(s32[8,64]{1,0:T(8,128)} %param.8) | copy-start | bytes 6148
  87.9 15.2 %collective-permute-start.1 = (f32[2,2,4,64,128]{4,3,2,0,1:T(8,128)S(1)}, f32[2,2,4,64,128]{4,3,2,0,1:T(8,128)S(1)}, u32[]{:S(2)}, u32[]{:S(2)}) collective-permute-start(f32[2,2,4,64,128]{4,3,2,0,1:T(8,128)S(1)} %bitcast.145), channel_id=1, source_target_pairs={{0,2},{1,3},{2,0},{3,1},{4,6},{5,7},{6,4},{7,5},{8,10},{9,11},{10,... | collective-permute-start | bytes 1572872 | tf_op jit(solution)/shard_map/ppermute | solution.py:254
  91.0 14.0 %collective-permute-start.4 = (f32[2,2,4,64,128]{4,3,2,0,1:T(8,128)S(1)}, f32[2,2,4,64,128]{4,3,2,0,1:T(8,128)S(1)}, u32[]{:S(2)}, u32[]{:S(2)}) collective-permute-start(f32[2,2,4,64,128]{4,3,2,0,1:T(8,128)S(1)} %bitcast.146), channel_id=1, source_target_pairs={{0,4},{1,5},{2,6},{3,7},{4,0},{5,1},{6,2},{7,3},{8,12},{9,13},{10,... | collective-permute-start | bytes 1572872 | tf_op jit(solution)/shard_map/ppermute | solution.py:254
  103.1 7.9 %collective-permute-start.2 = (f32[2,4,64,128]{3,2,1,0:T(8,128)S(1)}, f32[2,4,64,128]{3,2,1,0:T(8,128)S(1)}, u32[]{:S(2)}, u32[]{:S(2)}) collective-permute-start(f32[2,4,64,128]{3,2,1,0:T(8,128)S(1)} %dynamic-slice_bitcast_fusion.2), channel_id=1, source_target_pairs={{0,4},{1,5},{2,6},{3,7},{4,0},{5,1},{6,2},{7,3},{8,12},{9,13},{10,... | collective-permute-start | bytes 786440 | tf_op jit(solution)/shard_map/ppermute | solution.py:254
  105.1 8.6 %collective-permute-start.5 = (f32[2,4,64,128]{3,2,1,0:T(8,128)S(1)}, f32[2,4,64,128]{3,2,1,0:T(8,128)S(1)}, u32[]{:S(2)}, u32[]{:S(2)}) collective-permute-start(f32[2,4,64,128]{3,2,1,0:T(8,128)S(1)} %dynamic-slice_bitcast_fusion.1), channel_id=1, source_target_pairs={{0,2},{1,3},{2,0},{3,1},{4,6},{5,7},{6,4},{7,5},{8,10},{9,11},{10,... | collective-permute-start | bytes 786440 | tf_op jit(solution)/shard_map/ppermute | solution.py:254
  111.1 11.6 %collective-permute-start.3 = (f32[4,64,128]{2,1,0:T(8,128)S(1)}, f32[4,64,128]{2,1,0:T(8,128)S(1)}, u32[]{:S(2)}, u32[]{:S(2)}) collective-permute-start(f32[4,64,128]{2,1,0:T(8,128)S(1)} %dynamic-slice_bitcast_fusion.4), channel_id=1, source_target_pairs={{0,8},{1,9},{2,10},{3,11},{4,12},{5,13},{6,14},{7,15},{8,0},{9,1},... | collective-permute-start | bytes 393224 | tf_op jit(solution)/shard_map/ppermute | solution.py:254
  113.7 10.9 %collective-permute-start.6 = (f32[4,64,128]{2,1,0:T(8,128)S(1)}, f32[4,64,128]{2,1,0:T(8,128)S(1)}, u32[]{:S(2)}, u32[]{:S(2)}) collective-permute-start(f32[4,64,128]{2,1,0:T(8,128)S(1)} %dynamic-slice_bitcast_fusion.3), channel_id=1, source_target_pairs={{0,8},{1,9},{2,10},{3,11},{4,12},{5,13},{6,14},{7,15},{8,0},{9,1},... | collective-permute-start | bytes 393224 | tf_op jit(solution)/shard_map/ppermute | solution.py:254

commit v3 on v2

--- a/solution.py
+++ b/solution.py
@@ -138,9 +138,10 @@
     cos_part, sin_part = twiddle_parts()
     cos_part = cos_part[:, :, None]
     sin_part = sin_part[:, :, None]
-    real_part = section_one[:, 0] * cos_part + section_one[:, 1] * sin_part
-    imag_part = section_one[:, 1] * cos_part - section_one[:, 0] * sin_part
-    section_one = jnp.stack([real_part, imag_part], 1).astype(jnp.bfloat16)
+    signs = jnp.array([1.0, -1.0], jnp.float32)[None, :, None, None, None]
+    section_one = (
+        section_one * cos_part[None, None] + section_one[:, ::-1] * (signs * sin_part[None, None])
+    ).astype(jnp.bfloat16)
     section_two = jnp.einsum(
         "sckma,cmdj->sdkja", section_one, dft_table(FB), preferred_element_type=jnp.float32
     )

time: 165 us -> 179 us (1.085)
  other arithmetic: 20 us -> 29 us
  matrix products: 34.8 us -> 39.3 us
    convert_element_type x0 -> x1, other arithmetic: none -> 14.2 us  [spectra(): section_one = (section_one * cos_part[None, None] + section_one[:, ::-1]...]
    another operation x1 -> x0, local copies, waits for them, and re-layouts: 9.18 us -> none  [spectra(): section_one = jnp.stack([real_part, imag_part], 1).astype(jnp.bfloat16)]
    convert_element_type x0 -> x1, local copies, waits for them, and re-layouts: none -> 9.12 us  [spectra(): section_one = (section_one * cos_part[None, None] + section_one[:, ::-1]...]
    another operation x7 -> x5, other arithmetic: 7.81 us -> 2.43 us
    dot_general x1, matrix products: 4.62 us -> 9.14 us  [spectra(): jnp.einsum('ascnm,cndk->sdkma', shaped, dft_table(FA), preferred_element_...]
    unnamed x14 -> x16, local copies, waits for them, and re-layouts: 4.88 us -> 4.84 us
where the time goes in v3:
time: 179 us; the launch traced here: 178 us
  matrix products  39.3 us (22%)
  local copies, waits for them, and re-layouts  33.5 us (19%)
  other arithmetic  29 us (16%)
  waiting for transfers between devices  28.2 us (16%)
  Pallas kernels  22.1 us (12%)
  blocking collectives  13.1 us (7%)
  starting transfers between devices  12.5 us (7%)
    ppermute x7, waiting for transfers between devices, halve(): lax.ppermute(send, 'fh', perm=pairs)  28.2 us
    pallas_call x1, Pallas kernels, spd_solve(): pl.pallas_call(_solve_body, out_shape=jax.ShapeDtypeStruct(rhs.shape, jnp...  22.1 us
    convert_element_type x1, other arithmetic, spectra(): section_one = (section_one * cos_part[None, None] + section_one[:, ::-1]...  14.2 us
    all_to_all x1, blocking collectives, on_device(): return lax.all_to_all(result, 'fh', split_axis=0, concat_axis=3, tiled=True)  13.1 us
    ppermute x7, starting transfers between devices, halve(): lax.ppermute(send, 'fh', perm=pairs)  12.5 us
    reshape x1, local copies, waits for them, and re-layouts, spectra(): shaped = samples.reshape(antennas_here, symbol_count, 2, FA, FB)  10.9 us
    dot_general x1, matrix products, spectra(): jnp.einsum('ascnm,cndk->sdkma', shaped, dft_table(FA), preferred_element_...  9.14 us
    convert_element_type x1, local copies, waits for them, and re-layouts, spectra(): section_one = (section_one * cos_part[None, None] + section_one[:, ::-1]...  9.12 us
  transfers between devices with their start and end apart: 7, of which 5 were waited for; matrix products, arithmetic and copies ran while one was open for 0% of the time, Pallas kernels for 0%

profile of v3, /device:TPU:0, one launch (start us, length us, event | category | flops | bytes accessed | tf_op | source)
XLA Modules:
  0.0 178.0 jit_solution(13741355724572737248)
XLA Ops:
  0.0 0.1 negate_convert_fusion.2
  0.1 0.1 fusion.56
  0.1 0.1 sine_multiply_fusion.1
  0.2 0.1 cosine_multiply_fusion
  0.3 1.1 negate_convert_fusion
  1.4 1.0 fusion.33
  2.4 0.0 copy-start.6
  2.4 10.9 %reshape.345 = bf16[128,3,2,16,256,1]{4,3,2,1,0,5:T(8,128)(2,1)} reshape(bf16[128,3,2,4096]{3,2,1,0:T(2,128)(2,1)} %param.6) | data formatting | bytes 12582912 | tf_op jit(solution)/shard_map/reshape | solution.py:134
  13.3 0.1 broadcast_multiply_fusion
  13.4 9.1 %convolution_bitcast_fusion = f32[3,2,16,256,128]{3,2,0,4,1:T(8,128)} fusion(bf16[128,3,2,16,256,1]{4,3,2,1,0,5:T(8,128)(2,1)} %reshape.345, bf16[1,16,2,16]{1,3,0,2:T(8,128)(2,1)S(1)} %get-tuple-element.23, bf16[1,16,2,16]{1,3,0,2:T(8,128)(2,1)S(1)} %get-tuple-element.22), kind=kOutput, calls=%fused_computation.6 | convolution fusion | flops 201330688 | bytes 18876416 | tf_op jit(solution)/shard_map/ascnm,cndk->sdkma/dot_general | solution.py:135
  22.5 14.2 %add_convert_fusion = bf16[3,2,16,256,128]{3,2,0,4,1:T(8,128)(2,1)} fusion(f32[3,2,16,256,128]{3,2,0,4,1:T(8,128)} %convolution_bitcast_fusion, f32[2,16,256]{2,1,0:T(8,128)S(1)} %broadcast_multiply_fusion, f32[16,256]{1,0:T(8,128)S(1)} %cosine_multiply_fusion), kind=kLoop, calls=%fused_computation.1 | loop fusion | flops 12582912 | bytes 18923520 | tf_op jit(solution)/shard_map/convert_element_type | solution.py:144
  36.8 9.1 %copy.100 = bf16[3,2,16,256,128]{4,3,1,2,0:T(8,128)(2,1)} copy(bf16[3,2,16,256,128]{3,2,0,4,1:T(8,128)(2,1)} %add_convert_fusion) | data formatting | bytes 12582912 | tf_op jit(solution)/shard_map/convert_element_type | solution.py:144
  45.9 6.7 %fusion = bf16[3,2,16,256,128]{4,3,2,0,1:T(8,128)(2,1)S(1)} fusion(bf16[3,2,16,256,128]{4,3,1,2,0:T(8,128)(2,1)} %copy.100, bf16[1,256,2,256]{1,3,0,2:T(8,128)(2,1)S(1)} %get-tuple-element.19, bf16[1,256,2,256]{1,3,0,2:T(8,128)(2,1)S(1)} %get-tuple-element.18), kind=kOutput, calls=%fused_computation.3 | convolution fusion | flops 3225419776 | bytes 13107200 | tf_op jit(solution)/shard_map/sckma,cmdj->sdkja/dot_general | solution.py:145
  52.6 0.3 slice.36
  52.9 2.3 %copy-done.2 = bf16[3,2,16,256,128]{4,3,2,0,1:T(8,128)(2,1)} copy-done((bf16[3,2,16,256,128]{4,3,2,0,1:T(8,128)(2,1)}, bf16[3,2,16,256,128]{4,3,2,0,1:T(8,128)(2,1)S(1)}, u32[]{:S(2)}) %copy-start.2) | copy-done | bytes 6291480
  55.2 0.1 iota_add_fusion
  55.3 0.1 broadcast_add_fusion
  55.4 0.5 copy-done.4
  55.9 0.2 fusion.40
  56.1 5.7 %fusion.4 = bf16[2,64,128,128,1,1,1]{3,1,6,5,2,0,4:T(8,128)(2,1)S(1)} fusion(bf16[2,2,16,128,2,128,1]{5,4,3,2,0,1,6:T(2,128)(2,1)S(1)} %bitcast.136, bf16[1,64,2,2,16,2]{1,4,2,3,0,5:T(8,128)(2,1)S(1)} %get-tuple-element.21, bf16[1,64,2,2,16,2]{1,4,2,3,0,5:T(8,128)(2,1)S(1)} %get-tuple-element.20), kind=kOutput, calls=%fused_computation.11 | convolution fusion | flops 536936448 | bytes 8421376 | tf_op jit(solution)/shard_map/tcarbm,dktcab->rdkm/dot_general | solution.py:216
  61.8 1.0 copy.160
  62.9 0.4 slice_negate_fusion
  63.3 1.6 slice-done
  64.9 1.4 copy.106
  66.3 3.3 %convolution_bitcast_fusion.1 = f32[128,64,32]{2,1,0:T(8,128)} fusion(bf16[128,2,32,128]{3,2,0,1:T(8,128)(2,1)S(1)} %bitcast.140, bf16[2,64,128,128,1,1,1]{3,1,6,5,2,0,4:T(8,128)(2,1)S(1)} %fusion.4), kind=kOutput, calls=%fused_computation.16 | convolution fusion | flops 134217728 | bytes 7340032 | tf_op jit(solution)/shard_map/rckm,rcum->rku/dot_general | solution.py:229
  69.6 3.2 %fusion.10 = f32[128,64,32]{2,1,0:T(8,128)} fusion(bf16[128,1,64,128]{3,2,1,0:T(8,128)(2,1)S(1)} %get-tuple-element.8, bf16[128,1,64,128]{3,2,1,0:T(8,128)(2,1)S(1)} %get-tuple-element.7, bf16[128,2,32,128]{3,2,0,1:T(8,128)(2,1)S(1)} %bitcast.141), kind=kOutput, calls=%fused_computation.15 | convolution fusion | flops 136314880 | bytes 7340032 | tf_op jit(solution)/shard_map/rckm,rcum->rku/dot_general | solution.py:230
  72.8 3.4 %fusion.9 = f32[128,64,64,1]{2,1,3,0:T(8,128)} fusion(bf16[128,1,64,128]{3,2,1,0:T(8,128)(2,1)S(1)} %get-tuple-element.8, bf16[128,1,64,128]{3,2,1,0:T(8,128)(2,1)S(1)} %get-tuple-element.7, bf16[2,64,128,128,1,1,1]{3,1,6,5,2,0,4:T(8,128)(2,1)S(1)} %fusion.4), kind=kOutput, calls=%fused_computation.14 | convolution fusion | flops 270532608 | bytes 10485760 | tf_op jit(solution)/shard_map/rckm,rclm->rkl/dot_general | solution.py:221
  76.2 7.9 %bitcast_select_fusion = f32[128,64,64]{2,1,0:T(8,128)} fusion(f32[128,64,64,1]{2,1,3,0:T(8,128)} %fusion.9, pred[64,64]{1,0:T(8,128)(4,1)S(1)} %iota_compare_fusion.3, bf16[2,64,128,128,1,1,1]{3,1,6,5,2,0,4:T(8,128)(2,1)} %copy-done), kind=kOutput, calls=%fused_computation.10 | convolution fusion | flops 268959744 | bytes 8392704 | tf_op jit(solution)/shard_map/rckm,rclm->rkl/dot_general | solution.py:220
  84.2 6.9 %pad_maximum_fusion.1 = f32[128,64,128]{2,1,0:T(8,128)S(1)} fusion(f32[128,64,32]{2,1,0:T(8,128)} %fusion.10, f32[128,64,32]{2,1,0:T(8,128)} %convolution_bitcast_fusion.1, f32[128,64,64]{2,1,0:T(8,128)} %bitcast_select_fusion), kind=kLoop, calls=%fused_computation.9 | loop fusion | flops 2097152 | bytes 8388608 | tf_op jit(solution)/shard_map/concatenate | solution.py:231
  91.0 1.9 %copy-done.1 = f32[128,64,128]{2,1,0:T(8,128)} copy-done((f32[128,64,128]{2,1,0:T(8,128)}, f32[128,64,128]{2,1,0:T(8,128)S(1)}, u32[]{:S(2)}) %copy-start.1) | copy-done | bytes 4194328
  93.0 1.5 dynamic-slice_bitcast_fusion
  94.5 0.5 collective-permute-start
  95.0 4.0 %collective-permute-done = f32[2,2,2,8,64,128]{5,4,3,2,1,0:T(8,128)S(1)} collective-permute-done((f32[2,2,2,8,64,128]{5,4,3,2,1,0:T(8,128)}, f32[2,2,2,8,64,128]{5,4,3,2,1,0:T(8,128)S(1)}, u32[]{:S(2)}, u32[]{:S(2)}) %collective-permute-start) | collective-permute-done | bytes 2097184 | tf_op jit(solution)/shard_map/ppermute | solution.py:255
  99.0 2.0 %bitcast_add_fusion = f32[2,2,2,8,64,128]{5,4,3,2,1,0:T(8,128)S(1)} fusion(f32[2,2,2,8,64,128]{5,4,3,2,1,0:T(8,128)S(1)} %collective-permute-done, f32[2,2,2,2,8,64,128]{6,5,4,3,2,1,0:T(8,128)} %bitcast.139, s32[]{:T(128)S(6)} %select_n.146), kind=kLoop, calls=%fused_computation.18 | loop fusion | flops 524288 | bytes 6291460 | tf_op jit(solution)/shard_map/add | solution.py:255
  100.9 0.0 copy-start.5
  100.9 0.0 copy-start.7
  101.0 0.2 fusion.64
  101.1 0.0 copy-start.3
  101.2 0.1 constant_dynamic-slice_fusion.3
  101.3 3.0 %collective-permute-start.1 = (f32[2,2,4,64,128]{4,3,2,0,1:T(8,128)S(1)}, f32[2,2,4,64,128]{4,3,2,0,1:T(8,128)S(1)}, u32[]{:S(2)}, u32[]{:S(2)}) collective-permute-start(f32[2,2,4,64,128]{4,3,2,0,1:T(8,128)S(1)} %bitcast.145), channel_id=1, source_target_pairs={{0,2},{1,3},{2,0},{3,1},{4,6},{5,7},{6,4},{7,5},{8,10},{9,11},{10,... | collective-permute-start | bytes 1572872 | tf_op jit(solution)/shard_map/ppermute | solution.py:255
  104.3 0.1 constant_dynamic-slice_fusion.1
  104.4 1.6 collective-permute-start.4
  106.1 10.4 %collective-permute-done.1 = f32[2,2,4,64,128]{4,3,2,0,1:T(8,128)S(1)} collective-permute-done((f32[2,2,4,64,128]{4,3,2,0,1:T(8,128)S(1)}, f32[2,2,4,64,128]{4,3,2,0,1:T(8,128)S(1)}, u32[]{:S(2)}, u32[]{:S(2)}) %collective-permute-start.1) | collective-permute-done | bytes 524320 | tf_op jit(solution)/shard_map/ppermute | solution.py:255
  116.5 0.1 bitcast_add_fusion.2
  116.6 1.9 %collective-permute-start.2 = (f32[2,4,64,128]{3,2,1,0:T(8,128)S(1)}, f32[2,4,64,128]{3,2,1,0:T(8,128)S(1)}, u32[]{:S(2)}, u32[]{:S(2)}) collective-permute-start(f32[2,4,64,128]{3,2,1,0:T(8,128)S(1)} %dynamic-slice_bitcast_fusion.2), channel_id=1, source_target_pairs={{0,4},{1,5},{2,6},{3,7},{4,0},{5,1},{6,2},{7,3},{8,12},{9,13},{10,... | collective-permute-start | bytes 786440 | tf_op jit(solution)/shard_map/ppermute | solution.py:255
  118.4 0.1 bitcast_add_fusion.1
  118.5 1.6 collective-permute-start.5
  120.1 4.3 %collective-permute-done.2 = f32[2,4,64,128]{3,2,1,0:T(8,128)S(1)} collective-permute-done((f32[2,4,64,128]{3,2,1,0:T(8,128)S(1)}, f32[2,4,64,128]{3,2,1,0:T(8,128)S(1)}, u32[]{:S(2)}, u32[]{:S(2)}) %collective-permute-start.2) | collective-permute-done | bytes 262176 | tf_op jit(solution)/shard_map/ppermute | solution.py:255
  124.6 2.6 %collective-permute-start.3 = (f32[4,64,128]{2,1,0:T(8,128)S(1)}, f32[4,64,128]{2,1,0:T(8,128)S(1)}, u32[]{:S(2)}, u32[]{:S(2)}) collective-permute-start(f32[4,64,128]{2,1,0:T(8,128)S(1)} %dynamic-slice_bitcast_fusion.4), channel_id=1, source_target_pairs={{0,8},{1,9},{2,10},{3,11},{4,12},{5,13},{6,14},{7,15},{8,0},{9,1},... | collective-permute-start | bytes 393224 | tf_op jit(solution)/shard_map/ppermute | solution.py:255
  127.1 0.0 collective-permute-done.5
  127.2 1.4 collective-permute-start.6
  128.6 7.6 %collective-permute-done.3 = f32[4,64,128]{2,1,0:T(8,128)S(1)} collective-permute-done((f32[4,64,128]{2,1,0:T(8,128)S(1)}, f32[4,64,128]{2,1,0:T(8,128)S(1)}, u32[]{:S(2)}, u32[]{:S(2)}) %collective-permute-start.3) | collective-permute-done | bytes 131104 | tf_op jit(solution)/shard_map/ppermute | solution.py:255
  136.2 1.9 %collective-permute-done.6 = f32[4,64,128]{2,1,0:T(8,128)S(1)} collective-permute-done((f32[4,64,128]{2,1,0:T(8,128)S(1)}, f32[4,64,128]{2,1,0:T(8,128)S(1)}, u32[]{:S(2)}, u32[]{:S(2)}) %collective-permute-start.6) | collective-permute-done | bytes 131104 | tf_op jit(solution)/shard_map/ppermute | solution.py:255
  138.1 0.1 copy.115
  138.3 0.3 fusion.17
  138.5 0.9 pad_maximum_fusion.6.b_ref
  139.4 0.2 fusion.62
  139.6 1.0 maximum_maximum_fusion.a_ref
  140.6 22.1 %shard_map.64 = f32[8,128,32]{2,1,0:T(8,128)} custom-call(f32[8,128,128]{2,1,0:T(8,128)} %maximum_maximum_fusion.a_ref, f32[8,128,32]{2,1,0:T(8,128)} %pad_maximum_fusion.6.b_ref), custom_call_target="tpu_custom_call" | custom-call | tf_op jit(solution)/shard_map/pallas_call | solution.py:100
  162.7 1.2 copy.116
  163.9 0.2 reshape.342
  164.1 0.1 copy.118
  164.3 13.1 %all_to_all.18 = f32[64,1,2,256]{3,2,1,0:T(2,128)S(1)} all-to-all(f32[64,1,2,256]{3,2,1,0:T(2,128)S(1)} %copy.118), channel_id=1, replica_groups=mesh['cells'=2,'fh'=16] {'fh'}, dimensions={0} | all-to-all | bytes 262144 | tf_op jit(solution)/shard_map/all_to_all | solution.py:289
  177.4 0.7 copy.143
  (33 shorter events, 0.4 us)
Async XLA Ops:
  2.4 10.9 %copy-start.6 = (f32[2]{0:T(128)S(1)}, f32[2]{0:T(128)}, u32[]{:S(2)}) copy-start(f32[2]{0:T(128)} %constant.138.clone) | copy-start | bytes 28
  52.6 2.6 %copy-start.2 = (bf16[3,2,16,256,128]{4,3,2,0,1:T(8,128)(2,1)}, bf16[3,2,16,256,128]{4,3,2,0,1:T(8,128)(2,1)S(1)}, u32[]{:S(2)}) copy-start(bf16[3,2,16,256,128]{4,3,2,0,1:T(8,128)(2,1)S(1)} %fusion) | copy-start | bytes 18874372
  55.2 0.7 copy-start.4
  61.8 11.0 %copy-start = (bf16[2,64,128,128,1,1,1]{3,1,6,5,2,0,4:T(8,128)(2,1)}, bf16[2,64,128,128,1,1,1]{3,1,6,5,2,0,4:T(8,128)(2,1)S(1)}, u32[]{:S(2)}) copy-start(bf16[2,64,128,128,1,1,1]{3,1,6,5,2,0,4:T(8,128)(2,1)S(1)} %fusion.4) | copy-start | bytes 12582916
  62.8 2.0 %slice-start = ((bf16[3,2,16,256,128]{4,3,2,0,1:T(8,128)(2,1)}), bf16[1,2,16,256,128]{4,3,2,0,1:T(8,128)(2,1)S(1)}, s32[]{:S(2)}) async-start(bf16[3,2,16,256,128]{4,3,2,0,1:T(8,128)(2,1)} %copy-done.2), calls=%async_computation.1 | async-start | bytes 4194304 | tf_op jit(solution)/shard_map/slice | solution.py:283
  91.0 2.0 %copy-start.1 = (f32[128,64,128]{2,1,0:T(8,128)}, f32[128,64,128]{2,1,0:T(8,128)S(1)}, u32[]{:S(2)}) copy-start(f32[128,64,128]{2,1,0:T(8,128)S(1)} %pad_maximum_fusion.1) | copy-start | bytes 12582916
  94.5 4.5 %collective-permute-start = (f32[2,2,2,8,64,128]{5,4,3,2,1,0:T(8,128)}, f32[2,2,2,8,64,128]{5,4,3,2,1,0:T(8,128)S(1)}, u32[]{:S(2)}, u32[]{:S(2)}) collective-permute-start(f32[2,2,2,8,64,128]{5,4,3,2,1,0:T(8,128)} %dynamic-slice_bitcast_fusion), channel_id=1, source_target_pairs={{0,1},{1,0},{2,3},{3,2},{4,5},{5,4},{6,7},{7,6},{8,9},{9,8},{10,11... | collective-permute-start | bytes 6291464 | tf_op jit(solution)/shard_map/ppermute | solution.py:255
  100.9 3.3 %copy-start.5 = (f32[64]{0:T(128)S(1)}, f32[64]{0:T(128)}, u32[]{:S(2)}) copy-start(f32[64]{0:T(128)} %param.10) | copy-start | bytes 772
  100.9 3.3 %copy-start.7 = (s32[64]{0:T(128)S(1)}, s32[64]{0:T(128)}, u32[]{:S(2)}) copy-start(s32[64]{0:T(128)} %param.8) | copy-start | bytes 772
  101.1 4.9 %copy-start.3 = (s32[8,64]{1,0:T(8,128)S(1)}, s32[8,64]{1,0:T(8,128)}, u32[]{:S(2)}) copy-start(s32[8,64]{1,0:T(8,128)} %param.9) | copy-start | bytes 6148
  101.3 15.2 %collective-permute-start.1 = (f32[2,2,4,64,128]{4,3,2,0,1:T(8,128)S(1)}, f32[2,2,4,64,128]{4,3,2,0,1:T(8,128)S(1)}, u32[]{:S(2)}, u32[]{:S(2)}) collective-permute-start(f32[2,2,4,64,128]{4,3,2,0,1:T(8,128)S(1)} %bitcast.145), channel_id=1, source_target_pairs={{0,2},{1,3},{2,0},{3,1},{4,6},{5,7},{6,4},{7,5},{8,10},{9,11},{10,... | collective-permute-start | bytes 1572872 | tf_op jit(solution)/shard_map/ppermute | solution.py:255
  104.4 14.0 %collective-permute-start.4 = (f32[2,2,4,64,128]{4,3,2,0,1:T(8,128)S(1)}, f32[2,2,4,64,128]{4,3,2,0,1:T(8,128)S(1)}, u32[]{:S(2)}, u32[]{:S(2)}) collective-permute-start(f32[2,2,4,64,128]{4,3,2,0,1:T(8,128)S(1)} %bitcast.146), channel_id=1, source_target_pairs={{0,4},{1,5},{2,6},{3,7},{4,0},{5,1},{6,2},{7,3},{8,12},{9,13},{10,... | collective-permute-start | bytes 1572872 | tf_op jit(solution)/shard_map/ppermute | solution.py:255
  116.6 7.9 %collective-permute-start.2 = (f32[2,4,64,128]{3,2,1,0:T(8,128)S(1)}, f32[2,4,64,128]{3,2,1,0:T(8,128)S(1)}, u32[]{:S(2)}, u32[]{:S(2)}) collective-permute-start(f32[2,4,64,128]{3,2,1,0:T(8,128)S(1)} %dynamic-slice_bitcast_fusion.2), channel_id=1, source_target_pairs={{0,4},{1,5},{2,6},{3,7},{4,0},{5,1},{6,2},{7,3},{8,12},{9,13},{10,... | collective-permute-start | bytes 786440 | tf_op jit(solution)/shard_map/ppermute | solution.py:255
  118.5 8.6 %collective-permute-start.5 = (f32[2,4,64,128]{3,2,1,0:T(8,128)S(1)}, f32[2,4,64,128]{3,2,1,0:T(8,128)S(1)}, u32[]{:S(2)}, u32[]{:S(2)}) collective-permute-start(f32[2,4,64,128]{3,2,1,0:T(8,128)S(1)} %dynamic-slice_bitcast_fusion.1), channel_id=1, source_target_pairs={{0,2},{1,3},{2,0},{3,1},{4,6},{5,7},{6,4},{7,5},{8,10},{9,11},{10,... | collective-permute-start | bytes 786440 | tf_op jit(solution)/shard_map/ppermute | solution.py:255
  124.6 11.6 %collective-permute-start.3 = (f32[4,64,128]{2,1,0:T(8,128)S(1)}, f32[4,64,128]{2,1,0:T(8,128)S(1)}, u32[]{:S(2)}, u32[]{:S(2)}) collective-permute-start(f32[4,64,128]{2,1,0:T(8,128)S(1)} %dynamic-slice_bitcast_fusion.4), channel_id=1, source_target_pairs={{0,8},{1,9},{2,10},{3,11},{4,12},{5,13},{6,14},{7,15},{8,0},{9,1},... | collective-permute-start | bytes 393224 | tf_op jit(solution)/shard_map/ppermute | solution.py:255
  127.2 10.9 %collective-permute-start.6 = (f32[4,64,128]{2,1,0:T(8,128)S(1)}, f32[4,64,128]{2,1,0:T(8,128)S(1)}, u32[]{:S(2)}, u32[]{:S(2)}) collective-permute-start(f32[4,64,128]{2,1,0:T(8,128)S(1)} %dynamic-slice_bitcast_fusion.3), channel_id=1, source_target_pairs={{0,8},{1,9},{2,10},{3,11},{4,12},{5,13},{6,14},{7,15},{8,0},{9,1},... | collective-permute-start | bytes 393224 | tf_op jit(solution)/shard_map/ppermute | solution.py:255

commit v4 on v2

--- a/solution.py
+++ b/solution.py
@@ -225,9 +225,10 @@
     blocks = channel.shape[0]
     data_rows = jnp.transpose(data_part, (3, 1, 0, 2, 4, 5))
     data_rows = data_rows.reshape(blocks, 2, -1, data_rows.shape[-1])
-    matched_real = jnp.einsum("rckm,rcum->rku", channel, data_rows, preferred_element_type=jnp.float32)
-    matched_imag = jnp.einsum("rckm,rcum->rku", turned, data_rows, preferred_element_type=jnp.float32)
-    return jnp.concatenate([packed, matched_real, matched_imag], 2)
+    data_turned = jnp.stack([data_rows[:, 1], -data_rows[:, 0]], 1)
+    data_both = jnp.concatenate([data_rows, data_turned], axis=2)
+    matched = jnp.einsum("rckm,rcum->rku", channel, data_both, preferred_element_type=jnp.float32)
+    return jnp.concatenate([packed, matched], 2)
 
 
 def unpack_terms(terms, user_count):

time: 165 us -> 157 us (0.952)
  matrix products: 34.8 us -> 27.8 us
    dot_general x1, matrix products: 7.92 us -> 3.28 us  [packed_terms(): jnp.einsum('rckm,rclm->rkl', channel, channel, preferred_element_type=jnp...]
    concatenate x1, other arithmetic: 6.88 us -> 3.11 us  [packed_terms(): return jnp.concatenate([packed, matched], 2)]
    neg x1, other arithmetic: 0.41 us -> 2.37 us  [packed_terms(): turned = jnp.stack([-channel[:, 1], channel[:, 0]], 1)]
    dot_general x1, matrix products: 3.41 us -> 1.64 us  [packed_terms(): jnp.einsum('rckm,rclm->rkl', turned, channel, preferred_element_type=jnp....]
    squeeze x5, local copies, waits for them, and re-layouts: 1.59 us -> 3.3 us  [halve(): send = lax.dynamic_index_in_dim(parts, 1 - mine, axis=axis, keepdims=False)]
    unnamed x14 -> x22, local copies, waits for them, and re-layouts: 4.88 us -> 3.84 us
    dot_general x2 -> x1, matrix products: 6.48 us -> 6.01 us  [packed_terms(): jnp.einsum('rckm,rcum->rku', channel, data_both, preferred_element_type=j...]
where the time goes in v4:
time: 157 us; the launch traced here: 156 us
  local copies, waits for them, and re-layouts  33 us (21%)
  waiting for transfers between devices  28.1 us (18%)
  matrix products  27.8 us (18%)
  Pallas kernels  22.1 us (14%)
  other arithmetic  19.4 us (12%)
  blocking collectives  13.1 us (8%)
  starting transfers between devices  12.6 us (8%)
    ppermute x7, waiting for transfers between devices, halve(): lax.ppermute(send, 'fh', perm=pairs)  28.1 us
    pallas_call x1, Pallas kernels, spd_solve(): pl.pallas_call(_solve_body, out_shape=jax.ShapeDtypeStruct(rhs.shape, jnp...  22.1 us
    all_to_all x1, blocking collectives, on_device(): return lax.all_to_all(result, 'fh', split_axis=0, concat_axis=3, tiled=True)  13.1 us
    ppermute x7, starting transfers between devices, halve(): lax.ppermute(send, 'fh', perm=pairs)  12.6 us
    reshape x1, local copies, waits for them, and re-layouts, spectra(): shaped = samples.reshape(antennas_here, symbol_count, 2, FA, FB)  10.8 us
    another operation x1, local copies, waits for them, and re-layouts, spectra(): section_one = jnp.stack([real_part, imag_part], 1).astype(jnp.bfloat16)  9.1 us
    dot_general x1, matrix products, spectra(): jnp.einsum('sckma,cmdj->sdkja', section_one, dft_table(FB), preferred_ele...  6.61 us
    dot_general x1, matrix products, packed_terms(): jnp.einsum('rckm,rcum->rku', channel, data_both, preferred_element_type=j...  6.01 us
  transfers between devices with their start and end apart: 7, of which 5 were waited for; matrix products, arithmetic and copies ran while one was open for 0% of the time, Pallas kernels for 0%

profile of v4, /device:TPU:0, one launch (start us, length us, event | category | flops | bytes accessed | tf_op | source)
XLA Modules:
  0.0 156.4 jit_solution(12173092557739212089)
XLA Ops:
  0.0 0.1 negate_convert_fusion.2
  0.1 0.1 fusion.62
  0.1 0.1 sine_multiply_fusion.1
  0.2 1.1 negate_convert_fusion
  1.3 1.0 fusion.39
  2.3 10.8 %reshape.338 = bf16[128,3,2,16,256,1]{4,3,2,1,0,5:T(8,128)(2,1)} reshape(bf16[128,3,2,4096]{3,2,1,0:T(2,128)(2,1)} %param.5) | data formatting | bytes 12582912 | tf_op jit(solution)/shard_map/reshape | solution.py:134
  13.1 4.6 %convolution_bitcast_fusion = f32[3,2,16,256,128]{3,2,0,4,1:T(8,128)S(1)} fusion(bf16[128,3,2,16,256,1]{4,3,2,1,0,5:T(8,128)(2,1)} %reshape.338, bf16[1,16,2,16]{1,3,0,2:T(8,128)(2,1)S(1)} %get-tuple-element.27, bf16[1,16,2,16]{1,3,0,2:T(8,128)(2,1)S(1)} %get-tuple-element.26), kind=kOutput, calls=%fused_computation.8 | convolution fusion | flops 201330688 | bytes 18876416 | tf_op jit(solution)/shard_map/ascnm,cndk->sdkma/dot_general | solution.py:135
  17.8 2.2 %add_convert_fusion = (bf16[3,1,16,256,128]{3,2,0,4,1:T(8,128)(2,1)S(1)}, bf16[3,1,16,256,128]{3,2,0,4,1:T(8,128)(2,1)S(1)}) fusion(f32[3,2,16,256,128]{3,2,0,4,1:T(8,128)S(1)} %convolution_bitcast_fusion, f32[16,256]{1,0:T(8,128)S(1)} %get-tuple-element.33, f32[16,256]{1,0:T(8,128)S(1)} %get-tuple-element.34), kind=kLoop, calls=%fused_computation.7 | loop fusion | flops 12582912 | bytes 18907136 | tf_op jit(solution)/shard_map/convert
  20.0 3.2 %pad_maximum_fusion = bf16[3,2,16,256,128]{3,2,0,4,1:T(8,128)(2,1)} fusion(bf16[3,1,16,256,128]{3,2,0,4,1:T(8,128)(2,1)S(1)} %get-tuple-element.8, bf16[3,1,16,256,128]{3,2,0,4,1:T(8,128)(2,1)S(1)} %get-tuple-element.7), kind=kLoop, calls=%fused_computation.3 | loop fusion | flops 3145728 | bytes 12582912 | tf_op jit(solution)/shard_map/stack | solution.py:143
  23.1 9.1 %copy.87 = bf16[3,2,16,256,128]{4,3,1,2,0:T(8,128)(2,1)} copy(bf16[3,2,16,256,128]{3,2,0,4,1:T(8,128)(2,1)} %pad_maximum_fusion) | data formatting | bytes 12582912 | tf_op jit(solution)/shard_map/stack | solution.py:143
  32.3 6.6 %fusion = bf16[3,2,16,256,128]{4,3,2,0,1:T(8,128)(2,1)S(1)} fusion(bf16[3,2,16,256,128]{4,3,1,2,0:T(8,128)(2,1)} %copy.87, bf16[1,256,2,256]{1,3,0,2:T(8,128)(2,1)S(1)} %get-tuple-element.23, bf16[1,256,2,256]{1,3,0,2:T(8,128)(2,1)S(1)} %get-tuple-element.22), kind=kOutput, calls=%fused_computation.2 | convolution fusion | flops 3225419776 | bytes 13107200 | tf_op jit(solution)/shard_map/sckma,cmdj->sdkja/dot_general | solution.py:144
  38.9 0.0 copy-start.8
  38.9 0.3 slice.56
  39.2 0.1 iota_add_fusion
  39.3 0.1 broadcast_add_fusion
  39.4 0.2 copy-done.8
  39.6 0.2 fusion.46
  39.9 5.7 %fusion.8 = bf16[2,64,128,128,1,1,1]{3,1,6,5,2,0,4:T(8,128)(2,1)S(1)} fusion(bf16[2,2,16,128,2,128,1]{5,4,3,2,0,1,6:T(2,128)(2,1)S(1)} %bitcast.135, bf16[1,64,2,2,16,2]{1,4,2,3,0,5:T(8,128)(2,1)S(1)} %get-tuple-element.25, bf16[1,64,2,2,16,2]{1,4,2,3,0,5:T(8,128)(2,1)S(1)} %get-tuple-element.24), kind=kOutput, calls=%fused_computation.17 | convolution fusion | flops 536936448 | bytes 8421376 | tf_op jit(solution)/shard_map/tcarbm,dktcab->rdkm/dot_general | solution.py:215
  45.5 1.4 copy.140
  46.9 1.3 copy-done
  48.2 3.3 %fusion.73 = f32[128,64,64,1]{2,1,3,0:T(8,128)} fusion(bf16[2,64,128,128,1,1,1]{3,1,6,5,2,0,4:T(8,128)(2,1)S(1)} %fusion.8), kind=kOutput, calls=%fused_computation.145 | convolution fusion | flops 268435456 | bytes 6291456 | tf_op jit(solution)/shard_map/rckm,rclm->rkl/dot_general | solution.py:219
  51.5 0.0 slice-start
  51.6 2.4 %slice_negate_fusion = (bf16[128,1,64,128]{3,2,1,0:T(8,128)(2,1)}, bf16[128,1,64,128]{3,2,1,0:T(8,128)(2,1)}) fusion(bf16[128,2,64,128]{3,2,1,0:T(8,128)(2,1)S(1)} %bitcast.138), kind=kLoop, calls=%fused_computation.22 | loop fusion | flops 1048576 | bytes 8388608 | tf_op jit(solution)/shard_map/neg | solution.py:218
  53.9 1.4 copy.93
  55.4 1.2 fusion.70
  56.6 6.0 %fusion.14 = f32[128,64,64]{2,1,0:T(8,128)} fusion(bf16[2,64,128,128,1,1,1]{3,1,6,5,2,0,4:T(8,128)(2,1)} %copy-done, bf16[128,1,32,128]{3,2,0,1:T(8,128)(2,1)} %get-tuple-element.14, bf16[128,1,32,128]{3,2,0,1:T(8,128)(2,1)S(1)} %get-tuple-element.13, bf16[128,2,32,128]{3,2,0,1:T(8,128)(2,1)S(1)} %bitcast.140), kind=kOutput, calls=%fused_computation.21 | convolution fusion | flops 281018368 | bytes 10485760 | tf_op jit(solution)/shard_map/rckm,rcum->rku/dot_general | solution.py:230
  62.6 1.1 copy-done.4
  63.8 0.6 copy-done.5
  64.4 1.6 %bitcast_select_fusion = f32[128,64,64]{2,1,0:T(8,128)S(1)} fusion(f32[128,64,64,1]{2,1,3,0:T(8,128)S(1)} %copy-done.2, bf16[128,1,64,128]{3,2,1,0:T(8,128)(2,1)S(1)} %copy-done.5, bf16[128,1,64,128]{3,2,1,0:T(8,128)(2,1)S(1)} %copy-done.4, pred[64,64]{1,0:T(8,128)(4,1)S(1)} %iota_compare_fusion.3, bf16[2,64,128,128,1,1,1]{3,1,6,5,2,0,4:T(8,128)(2,1)S(1)} %copy-done.1), kind=kOutput, calls=%fused_computation.16 | convolution fusion | flops 271056896 | bytes 12587008 | tf_op jit(solution)/shard_map/rckm,rclm->rkl/dot_general | solution.py:220
  66.0 0.5 copy-done.6
  66.6 3.1 %pad_maximum_fusion.1 = f32[128,64,128]{2,1,0:T(8,128)} fusion(f32[128,64,64]{2,1,0:T(8,128)S(1)} %copy-done.6, f32[128,64,64]{2,1,0:T(8,128)S(1)} %bitcast_select_fusion), kind=kLoop, calls=%fused_computation.15 | loop fusion | flops 1048576 | bytes 8388608 | tf_op jit(solution)/shard_map/concatenate | solution.py:231
  69.7 3.2 %dynamic-slice_bitcast_fusion = f32[2,2,2,8,64,128]{5,4,3,2,1,0:T(8,128)} fusion(f32[2,2,2,2,8,64,128]{6,5,4,3,2,1,0:T(8,128)} %bitcast.136, s32[]{:T(128)S(6)} %select_n.151), kind=kLoop, calls=%fused_computation.24 | loop fusion | bytes 4194308 | tf_op jit(solution)/shard_map/jit(dynamic_index_in_dim)/squeeze | solution.py:253
  72.9 0.5 collective-permute-start
  73.3 4.0 %collective-permute-done = f32[2,2,2,8,64,128]{5,4,3,2,1,0:T(8,128)S(1)} collective-permute-done((f32[2,2,2,8,64,128]{5,4,3,2,1,0:T(8,128)}, f32[2,2,2,8,64,128]{5,4,3,2,1,0:T(8,128)S(1)}, u32[]{:S(2)}, u32[]{:S(2)}) %collective-permute-start) | collective-permute-done | bytes 2097184 | tf_op jit(solution)/shard_map/ppermute | solution.py:255
  77.3 2.0 %bitcast_add_fusion = f32[2,2,2,8,64,128]{5,4,3,2,1,0:T(8,128)S(1)} fusion(f32[2,2,2,8,64,128]{5,4,3,2,1,0:T(8,128)S(1)} %collective-permute-done, f32[2,2,2,2,8,64,128]{6,5,4,3,2,1,0:T(8,128)} %bitcast.137, s32[]{:T(128)S(6)} %select_n.150), kind=kLoop, calls=%fused_computation.23 | loop fusion | flops 524288 | bytes 6291460 | tf_op jit(solution)/shard_map/add | solution.py:255
  79.3 0.0 copy-start.9
  79.3 0.0 copy-start.10
  79.3 0.2 fusion.69
  79.5 0.0 copy-start.7
  79.5 0.1 constant_dynamic-slice_fusion.1
  79.7 3.0 %collective-permute-start.4 = (f32[2,2,4,64,128]{4,3,2,0,1:T(8,128)S(1)}, f32[2,2,4,64,128]{4,3,2,0,1:T(8,128)S(1)}, u32[]{:S(2)}, u32[]{:S(2)}) collective-permute-start(f32[2,2,4,64,128]{4,3,2,0,1:T(8,128)S(1)} %bitcast.144), channel_id=1, source_target_pairs={{0,4},{1,5},{2,6},{3,7},{4,0},{5,1},{6,2},{7,3},{8,12},{9,13},{10,... | collective-permute-start | bytes 1572872 | tf_op jit(solution)/shard_map/ppermute | solution.py:255
  82.7 0.1 constant_dynamic-slice_fusion.3
  82.9 1.6 %collective-permute-start.1 = (f32[2,2,4,64,128]{4,3,2,0,1:T(8,128)S(1)}, f32[2,2,4,64,128]{4,3,2,0,1:T(8,128)S(1)}, u32[]{:S(2)}, u32[]{:S(2)}) collective-permute-start(f32[2,2,4,64,128]{4,3,2,0,1:T(8,128)S(1)} %bitcast.145), channel_id=1, source_target_pairs={{0,2},{1,3},{2,0},{3,1},{4,6},{5,7},{6,4},{7,5},{8,10},{9,11},{10,... | collective-permute-start | bytes 1572872 | tf_op jit(solution)/shard_map/ppermute | solution.py:255
  84.5 10.4 %collective-permute-done.4 = f32[2,2,4,64,128]{4,3,2,0,1:T(8,128)S(1)} collective-permute-done((f32[2,2,4,64,128]{4,3,2,0,1:T(8,128)S(1)}, f32[2,2,4,64,128]{4,3,2,0,1:T(8,128)S(1)}, u32[]{:S(2)}, u32[]{:S(2)}) %collective-permute-start.4) | collective-permute-done | bytes 524320 | tf_op jit(solution)/shard_map/ppermute | solution.py:255
  94.9 0.1 bitcast_add_fusion.1
  95.0 1.7 %collective-permute-start.5 = (f32[2,4,64,128]{3,2,1,0:T(8,128)S(1)}, f32[2,4,64,128]{3,2,1,0:T(8,128)S(1)}, u32[]{:S(2)}, u32[]{:S(2)}) collective-permute-start(f32[2,4,64,128]{3,2,1,0:T(8,128)S(1)} %dynamic-slice_bitcast_fusion.1), channel_id=1, source_target_pairs={{0,2},{1,3},{2,0},{3,1},{4,6},{5,7},{6,4},{7,5},{8,10},{9,11},{10,... | collective-permute-start | bytes 786440 | tf_op jit(solution)/shard_map/ppermute | solution.py:255
  96.8 0.1 bitcast_add_fusion.2
  96.9 1.6 %collective-permute-start.2 = (f32[2,4,64,128]{3,2,1,0:T(8,128)S(1)}, f32[2,4,64,128]{3,2,1,0:T(8,128)S(1)}, u32[]{:S(2)}, u32[]{:S(2)}) collective-permute-start(f32[2,4,64,128]{3,2,1,0:T(8,128)S(1)} %dynamic-slice_bitcast_fusion.2), channel_id=1, source_target_pairs={{0,4},{1,5},{2,6},{3,7},{4,0},{5,1},{6,2},{7,3},{8,12},{9,13},{10,... | collective-permute-start | bytes 786440 | tf_op jit(solution)/shard_map/ppermute | solution.py:255
  98.5 4.4 %collective-permute-done.5 = f32[2,4,64,128]{3,2,1,0:T(8,128)S(1)} collective-permute-done((f32[2,4,64,128]{3,2,1,0:T(8,128)S(1)}, f32[2,4,64,128]{3,2,1,0:T(8,128)S(1)}, u32[]{:S(2)}, u32[]{:S(2)}) %collective-permute-start.5) | collective-permute-done | bytes 262176 | tf_op jit(solution)/shard_map/ppermute | solution.py:255
  103.0 2.5 %collective-permute-start.6 = (f32[4,64,128]{2,1,0:T(8,128)S(1)}, f32[4,64,128]{2,1,0:T(8,128)S(1)}, u32[]{:S(2)}, u32[]{:S(2)}) collective-permute-start(f32[4,64,128]{2,1,0:T(8,128)S(1)} %dynamic-slice_bitcast_fusion.3), channel_id=1, source_target_pairs={{0,8},{1,9},{2,10},{3,11},{4,12},{5,13},{6,14},{7,15},{8,0},{9,1},... | collective-permute-start | bytes 393224 | tf_op jit(solution)/shard_map/ppermute | solution.py:255
  105.6 1.7 %collective-permute-start.3 = (f32[4,64,128]{2,1,0:T(8,128)S(1)}, f32[4,64,128]{2,1,0:T(8,128)S(1)}, u32[]{:S(2)}, u32[]{:S(2)}) collective-permute-start(f32[4,64,128]{2,1,0:T(8,128)S(1)} %dynamic-slice_bitcast_fusion.4), channel_id=1, source_target_pairs={{0,8},{1,9},{2,10},{3,11},{4,12},{5,13},{6,14},{7,15},{8,0},{9,1},... | collective-permute-start | bytes 393224 | tf_op jit(solution)/shard_map/ppermute | solution.py:255
  107.2 7.6 %collective-permute-done.6 = f32[4,64,128]{2,1,0:T(8,128)S(1)} collective-permute-done((f32[4,64,128]{2,1,0:T(8,128)S(1)}, f32[4,64,128]{2,1,0:T(8,128)S(1)}, u32[]{:S(2)}, u32[]{:S(2)}) %collective-permute-start.6) | collective-permute-done | bytes 131104 | tf_op jit(solution)/shard_map/ppermute | solution.py:255
  114.8 1.7 %collective-permute-done.3 = f32[4,64,128]{2,1,0:T(8,128)S(1)} collective-permute-done((f32[4,64,128]{2,1,0:T(8,128)S(1)}, f32[4,64,128]{2,1,0:T(8,128)S(1)}, u32[]{:S(2)}, u32[]{:S(2)}) %collective-permute-start.3) | collective-permute-done | bytes 131104 | tf_op jit(solution)/shard_map/ppermute | solution.py:255
  116.6 0.3 fusion.23
  116.8 0.1 copy.99
  117.0 0.9 pad_maximum_fusion.2.b_ref
  117.8 0.2 fusion.67
  118.0 1.0 maximum_maximum_fusion.1.a_ref
  119.0 22.1 %shard_map.55 = f32[8,128,32]{2,1,0:T(8,128)} custom-call(f32[8,128,128]{2,1,0:T(8,128)} %maximum_maximum_fusion.1.a_ref, f32[8,128,32]{2,1,0:T(8,128)} %pad_maximum_fusion.2.b_ref), custom_call_target="tpu_custom_call" | custom-call | tf_op jit(solution)/shard_map/pallas_call | solution.py:100
  141.1 1.2 copy.100
  142.3 0.2 reshape.335
  142.5 0.1 copy.102
  142.7 13.1 %all_to_all.18 = f32[64,1,2,256]{3,2,1,0:T(2,128)S(1)} all-to-all(f32[64,1,2,256]{3,2,1,0:T(2,128)S(1)} %copy.102), channel_id=1, replica_groups=mesh['cells'=2,'fh'=16] {'fh'}, dimensions={0} | all-to-all | bytes 262144 | tf_op jit(solution)/shard_map/all_to_all | solution.py:289
  155.7 0.7 copy.123
  (38 shorter events, 0.4 us)
Async XLA Ops:
  38.9 12.6 %copy-start.3 = (bf16[3,2,16,256,128]{4,3,2,0,1:T(8,128)(2,1)}, bf16[3,2,16,256,128]{4,3,2,0,1:T(8,128)(2,1)S(1)}, u32[]{:S(2)}) copy-start(bf16[3,2,16,256,128]{4,3,2,0,1:T(8,128)(2,1)S(1)} %fusion) | copy-start | bytes 18874372
  38.9 0.7 copy-start.8
  45.5 2.7 %copy-start = (bf16[2,64,128,128,1,1,1]{3,1,6,5,2,0,4:T(8,128)(2,1)}, bf16[2,64,128,128,1,1,1]{3,1,6,5,2,0,4:T(8,128)(2,1)S(1)}, u32[]{:S(2)}) copy-start(bf16[2,64,128,128,1,1,1]{3,1,6,5,2,0,4:T(8,128)(2,1)S(1)} %fusion.8) | copy-start | bytes 12582916
  51.5 2.4 %slice-start = ((bf16[3,2,16,256,128]{4,3,2,0,1:T(8,128)(2,1)}), bf16[1,2,16,256,128]{4,3,2,0,1:T(8,128)(2,1)S(1)}, s32[]{:S(2)}) async-start(bf16[3,2,16,256,128]{4,3,2,0,1:T(8,128)(2,1)} %copy-done.3), calls=%async_computation.1 | async-start | bytes 4194304 | tf_op jit(solution)/shard_map/slice | solution.py:283
  56.6 6.0 %copy-start.1 = (bf16[2,64,128,128,1,1,1]{3,1,6,5,2,0,4:T(8,128)(2,1)S(1)}, bf16[2,64,128,128,1,1,1]{3,1,6,5,2,0,4:T(8,128)(2,1)}, u32[]{:S(2)}) copy-start(bf16[2,64,128,128,1,1,1]{3,1,6,5,2,0,4:T(8,128)(2,1)} %copy-done) | copy-start | bytes 12582916
  56.6 6.0 %copy-start.2 = (f32[128,64,64,1]{2,1,3,0:T(8,128)S(1)}, f32[128,64,64,1]{2,1,3,0:T(8,128)}, u32[]{:S(2)}) copy-start(f32[128,64,64,1]{2,1,3,0:T(8,128)} %fusion.73) | copy-start | bytes 6291460
  56.6 7.1 %copy-start.4 = (bf16[128,1,64,128]{3,2,1,0:T(8,128)(2,1)S(1)}, bf16[128,1,64,128]{3,2,1,0:T(8,128)(2,1)}, u32[]{:S(2)}) copy-start(bf16[128,1,64,128]{3,2,1,0:T(8,128)(2,1)} %get-tuple-element.9) | copy-start | bytes 6291460
  56.6 7.7 %copy-start.5 = (bf16[128,1,64,128]{3,2,1,0:T(8,128)(2,1)S(1)}, bf16[128,1,64,128]{3,2,1,0:T(8,128)(2,1)}, u32[]{:S(2)}) copy-start(bf16[128,1,64,128]{3,2,1,0:T(8,128)(2,1)} %get-tuple-element.10) | copy-start | bytes 6291460
  64.4 2.2 %copy-start.6 = (f32[128,64,64]{2,1,0:T(8,128)S(1)}, f32[128,64,64]{2,1,0:T(8,128)}, u32[]{:S(2)}) copy-start(f32[128,64,64]{2,1,0:T(8,128)} %fusion.14) | copy-start | bytes 6291460
  72.9 4.5 %collective-permute-start = (f32[2,2,2,8,64,128]{5,4,3,2,1,0:T(8,128)}, f32[2,2,2,8,64,128]{5,4,3,2,1,0:T(8,128)S(1)}, u32[]{:S(2)}, u32[]{:S(2)}) collective-permute-start(f32[2,2,2,8,64,128]{5,4,3,2,1,0:T(8,128)} %dynamic-slice_bitcast_fusion), channel_id=1, source_target_pairs={{0,1},{1,0},{2,3},{3,2},{4,5},{5,4},{6,7},{7,6},{8,9},{9,8},{10,11... | collective-permute-start | bytes 6291464 | tf_op jit(solution)/shard_map/ppermute | solution.py:255
  79.3 3.4 %copy-start.9 = (f32[64]{0:T(128)S(1)}, f32[64]{0:T(128)}, u32[]{:S(2)}) copy-start(f32[64]{0:T(128)} %param.9) | copy-start | bytes 772
  79.3 3.4 %copy-start.10 = (s32[64]{0:T(128)S(1)}, s32[64]{0:T(128)}, u32[]{:S(2)}) copy-start(s32[64]{0:T(128)} %param.7) | copy-start | bytes 772
  79.5 4.9 %copy-start.7 = (s32[8,64]{1,0:T(8,128)S(1)}, s32[8,64]{1,0:T(8,128)}, u32[]{:S(2)}) copy-start(s32[8,64]{1,0:T(8,128)} %param.8) | copy-start | bytes 6148
  79.7 15.2 %collective-permute-start.4 = (f32[2,2,4,64,128]{4,3,2,0,1:T(8,128)S(1)}, f32[2,2,4,64,128]{4,3,2,0,1:T(8,128)S(1)}, u32[]{:S(2)}, u32[]{:S(2)}) collective-permute-start(f32[2,2,4,64,128]{4,3,2,0,1:T(8,128)S(1)} %bitcast.144), channel_id=1, source_target_pairs={{0,4},{1,5},{2,6},{3,7},{4,0},{5,1},{6,2},{7,3},{8,12},{9,13},{10,... | collective-permute-start | bytes 1572872 | tf_op jit(solution)/shard_map/ppermute | solution.py:255
  82.9 13.9 %collective-permute-start.1 = (f32[2,2,4,64,128]{4,3,2,0,1:T(8,128)S(1)}, f32[2,2,4,64,128]{4,3,2,0,1:T(8,128)S(1)}, u32[]{:S(2)}, u32[]{:S(2)}) collective-permute-start(f32[2,2,4,64,128]{4,3,2,0,1:T(8,128)S(1)} %bitcast.145), channel_id=1, source_target_pairs={{0,2},{1,3},{2,0},{3,1},{4,6},{5,7},{6,4},{7,5},{8,10},{9,11},{10,... | collective-permute-start | bytes 1572872 | tf_op jit(solution)/shard_map/ppermute | solution.py:255
  95.0 7.9 %collective-permute-start.5 = (f32[2,4,64,128]{3,2,1,0:T(8,128)S(1)}, f32[2,4,64,128]{3,2,1,0:T(8,128)S(1)}, u32[]{:S(2)}, u32[]{:S(2)}) collective-permute-start(f32[2,4,64,128]{3,2,1,0:T(8,128)S(1)} %dynamic-slice_bitcast_fusion.1), channel_id=1, source_target_pairs={{0,2},{1,3},{2,0},{3,1},{4,6},{5,7},{6,4},{7,5},{8,10},{9,11},{10,... | collective-permute-start | bytes 786440 | tf_op jit(solution)/shard_map/ppermute | solution.py:255
  96.9 8.6 %collective-permute-start.2 = (f32[2,4,64,128]{3,2,1,0:T(8,128)S(1)}, f32[2,4,64,128]{3,2,1,0:T(8,128)S(1)}, u32[]{:S(2)}, u32[]{:S(2)}) collective-permute-start(f32[2,4,64,128]{3,2,1,0:T(8,128)S(1)} %dynamic-slice_bitcast_fusion.2), channel_id=1, source_target_pairs={{0,4},{1,5},{2,6},{3,7},{4,0},{5,1},{6,2},{7,3},{8,12},{9,13},{10,... | collective-permute-start | bytes 786440 | tf_op jit(solution)/shard_map/ppermute | solution.py:255
  103.0 11.8 %collective-permute-start.6 = (f32[4,64,128]{2,1,0:T(8,128)S(1)}, f32[4,64,128]{2,1,0:T(8,128)S(1)}, u32[]{:S(2)}, u32[]{:S(2)}) collective-permute-start(f32[4,64,128]{2,1,0:T(8,128)S(1)} %dynamic-slice_bitcast_fusion.3), channel_id=1, source_target_pairs={{0,8},{1,9},{2,10},{3,11},{4,12},{5,13},{6,14},{7,15},{8,0},{9,1},... | collective-permute-start | bytes 393224 | tf_op jit(solution)/shard_map/ppermute | solution.py:255
  105.6 11.0 %collective-permute-start.3 = (f32[4,64,128]{2,1,0:T(8,128)S(1)}, f32[4,64,128]{2,1,0:T(8,128)S(1)}, u32[]{:S(2)}, u32[]{:S(2)}) collective-permute-start(f32[4,64,128]{2,1,0:T(8,128)S(1)} %dynamic-slice_bitcast_fusion.4), channel_id=1, source_target_pairs={{0,8},{1,9},{2,10},{3,11},{4,12},{5,13},{6,14},{7,15},{8,0},{9,1},... | collective-permute-start | bytes 393224 | tf_op jit(solution)/shard_map/ppermute | solution.py:255

commit v5 on v4

--- a/solution.py
+++ b/solution.py
@@ -215,10 +215,13 @@
     channel = jnp.einsum(
         "tcarbm,dktcab->rdkm", pilot_part, code_rows, preferred_element_type=jnp.float32
     ).astype(jnp.bfloat16)
-    turned = jnp.stack([-channel[:, 1], channel[:, 0]], 1)
-    gram_real = jnp.einsum("rckm,rclm->rkl", channel, channel, preferred_element_type=jnp.float32)
-    gram_imag = jnp.einsum("rckm,rclm->rkl", turned, channel, preferred_element_type=jnp.float32)
-    user_count = gram_real.shape[1]
+    mirrored = jnp.stack([channel[:, 1], -channel[:, 0]], 1)
+    gram = jnp.einsum(
+        "rckm,rclm->rkl", channel, jnp.concatenate([channel, mirrored], axis=2),
+        preferred_element_type=jnp.float32)
+    user_count = channel.shape[2]
+    gram_real = gram[:, :, :user_count]
+    gram_imag = gram[:, :, user_count:]
     row = lax.broadcasted_iota(jnp.int32, (user_count, user_count), 0)
     col = lax.broadcasted_iota(jnp.int32, (user_count, user_count), 1)
     packed = jnp.where(row <= col, gram_real, gram_imag)

time: 157 us -> 162 us (1.032)
  local copies, waits for them, and re-layouts: 33 us -> 36.1 us
    unnamed x22 -> x18, local copies, waits for them, and re-layouts: 3.84 us -> 6.98 us
    neg x1 -> x0, other arithmetic: 2.37 us -> none  [packed_terms(): turned = jnp.stack([-channel[:, 1], channel[:, 0]], 1)]
    slice x0 -> x1, other arithmetic: none -> 2.34 us  [packed_terms(): mirrored = jnp.stack([channel[:, 1], -channel[:, 0]], 1)]
    dot_general x2 -> x1, matrix products: 4.92 us -> 5.04 us  [packed_terms(): jnp.einsum('rckm,rclm->rkl', channel, jnp.concatenate([channel, mirrored]...]
where the time goes in v5:
time: 162 us; the launch traced here: 161 us
  local copies, waits for them, and re-layouts  36.1 us (22%)
  waiting for transfers between devices  28.3 us (17%)
  matrix products  27.9 us (17%)
  Pallas kernels  22.1 us (14%)
  other arithmetic  20.4 us (13%)
  blocking collectives  13.1 us (8%)
  starting transfers between devices  12.3 us (8%)
    ppermute x7, waiting for transfers between devices, halve(): lax.ppermute(send, 'fh', perm=pairs)  28.3 us
    pallas_call x1, Pallas kernels, spd_solve(): pl.pallas_call(_solve_body, out_shape=jax.ShapeDtypeStruct(rhs.shape, jnp...  22.1 us
    all_to_all x1, blocking collectives, on_device(): return lax.all_to_all(result, 'fh', split_axis=0, concat_axis=3, tiled=True)  13.1 us
    ppermute x7, starting transfers between devices, halve(): lax.ppermute(send, 'fh', perm=pairs)  12.3 us
    reshape x1, local copies, waits for them, and re-layouts, spectra(): shaped = samples.reshape(antennas_here, symbol_count, 2, FA, FB)  10.8 us
    another operation x1, local copies, waits for them, and re-layouts, spectra(): section_one = jnp.stack([real_part, imag_part], 1).astype(jnp.bfloat16)  9.14 us
    unnamed x18, local copies, waits for them, and re-layouts  6.98 us
    dot_general x1, matrix products, spectra(): jnp.einsum('sckma,cmdj->sdkja', section_one, dft_table(FB), preferred_ele...  6.68 us
  transfers between devices with their start and end apart: 7, of which 5 were waited for; matrix products, arithmetic and copies ran while one was open for 0% of the time, Pallas kernels for 0%

profile of v5, /device:TPU:0, one launch (start us, length us, event | category | flops | bytes accessed | tf_op | source)
XLA Modules:
  0.0 160.7 jit_solution(14742727720198436273)
XLA Ops:
  0.0 0.1 negate_convert_fusion.2
  0.1 0.1 fusion.65
  0.1 0.1 sine_multiply_fusion.1
  0.2 1.1 negate_convert_fusion
  1.3 1.0 fusion.42
  2.3 10.8 %reshape.338 = bf16[128,3,2,16,256,1]{4,3,2,1,0,5:T(8,128)(2,1)} reshape(bf16[128,3,2,4096]{3,2,1,0:T(2,128)(2,1)} %param.5) | data formatting | bytes 12582912 | tf_op jit(solution)/shard_map/reshape | solution.py:134
  13.2 4.7 %convolution_bitcast_fusion = f32[3,2,16,256,128]{3,2,0,4,1:T(8,128)S(1)} fusion(bf16[128,3,2,16,256,1]{4,3,2,1,0,5:T(8,128)(2,1)} %reshape.338, bf16[1,16,2,16]{1,3,0,2:T(8,128)(2,1)S(1)} %get-tuple-element.27, bf16[1,16,2,16]{1,3,0,2:T(8,128)(2,1)S(1)} %get-tuple-element.26), kind=kOutput, calls=%fused_computation.14 | convolution fusion | flops 201330688 | bytes 18876416 | tf_op jit(solution)/shard_map/ascnm,cndk->sdkma/dot_general | solution.py:135
  17.8 2.2 %add_convert_fusion = (bf16[3,1,16,256,128]{3,2,0,4,1:T(8,128)(2,1)S(1)}, bf16[3,1,16,256,128]{3,2,0,4,1:T(8,128)(2,1)S(1)}) fusion(f32[3,2,16,256,128]{3,2,0,4,1:T(8,128)S(1)} %convolution_bitcast_fusion, f32[16,256]{1,0:T(8,128)S(1)} %get-tuple-element.33, f32[16,256]{1,0:T(8,128)S(1)} %get-tuple-element.34), kind=kLoop, calls=%fused_computation.13 | loop fusion | flops 12582912 | bytes 18907136 | tf_op jit(solution)/shard_map/convert
  20.0 3.2 %pad_maximum_fusion = bf16[3,2,16,256,128]{3,2,0,4,1:T(8,128)(2,1)} fusion(bf16[3,1,16,256,128]{3,2,0,4,1:T(8,128)(2,1)S(1)} %get-tuple-element.8, bf16[3,1,16,256,128]{3,2,0,4,1:T(8,128)(2,1)S(1)} %get-tuple-element.7), kind=kLoop, calls=%fused_computation.9 | loop fusion | flops 3145728 | bytes 12582912 | tf_op jit(solution)/shard_map/stack | solution.py:143
  23.2 9.1 %copy.79 = bf16[3,2,16,256,128]{4,3,1,2,0:T(8,128)(2,1)} copy(bf16[3,2,16,256,128]{3,2,0,4,1:T(8,128)(2,1)} %pad_maximum_fusion) | data formatting | bytes 12582912 | tf_op jit(solution)/shard_map/stack | solution.py:143
  32.4 6.7 %fusion.6 = bf16[3,2,16,256,128]{4,3,2,0,1:T(8,128)(2,1)S(1)} fusion(bf16[3,2,16,256,128]{4,3,1,2,0:T(8,128)(2,1)} %copy.79, bf16[1,256,2,256]{1,3,0,2:T(8,128)(2,1)S(1)} %get-tuple-element.23, bf16[1,256,2,256]{1,3,0,2:T(8,128)(2,1)S(1)} %get-tuple-element.22), kind=kOutput, calls=%fused_computation.8 | convolution fusion | flops 3225419776 | bytes 13107200 | tf_op jit(solution)/shard_map/sckma,cmdj->sdkja/dot_general | solution.py:144
  39.1 0.0 copy-start
  39.1 2.6 %copy-done = bf16[3,2,16,256,128]{4,3,2,0,1:T(8,128)(2,1)} copy-done((bf16[3,2,16,256,128]{4,3,2,0,1:T(8,128)(2,1)}, bf16[3,2,16,256,128]{4,3,2,0,1:T(8,128)(2,1)S(1)}, u32[]{:S(2)}) %copy-start) | copy-done | bytes 6291480
  41.7 0.2 slice.69
  42.0 0.1 iota_add_fusion
  42.0 1.4 copy.83
  43.5 1.2 fusion.74
  44.6 0.1 broadcast_add_fusion
  44.7 0.2 fusion.49
  45.0 5.7 %fusion.10 = bf16[2,64,128,128,1,1,1]{3,1,6,5,2,0,4:T(8,128)(2,1)S(1)} fusion(bf16[2,2,16,128,2,128,1]{5,4,3,2,0,1,6:T(2,128)(2,1)S(1)} %bitcast.129, bf16[1,64,2,2,16,2]{1,4,2,3,0,5:T(8,128)(2,1)S(1)} %get-tuple-element.25, bf16[1,64,2,2,16,2]{1,4,2,3,0,5:T(8,128)(2,1)S(1)} %get-tuple-element.24), kind=kOutput, calls=%fused_computation.19 | convolution fusion | flops 536936448 | bytes 8421376 | tf_op jit(solution)/shard_map/tcarbm,dktcab->rdkm/dot_general | solution.py:215
  50.7 1.4 copy.125
  52.1 1.3 copy-done.1
  53.4 2.0 %copy-done.2 = bf16[2,64,128,128,1,1,1]{3,1,0,2,4,5,6:T(8,128)(2,1)} copy-done((bf16[2,64,128,128,1,1,1]{3,1,0,2,4,5,6:T(8,128)(2,1)}, bf16[2,64,128,128,1,1,1]{3,1,0,2,4,5,6:T(8,128)(2,1)S(1)}, u32[]{:S(2)}) %copy-start.2) | copy-done | bytes 4194328
  55.4 2.3 %fusion.72 = (bf16[128,1,64,128]{3,2,1,0:T(8,128)(2,1)}, bf16[128,1,64,128]{3,2,1,0:T(8,128)(2,1)}) fusion(bf16[128,2,64,128]{3,2,1,0:T(8,128)(2,1)S(1)} %bitcast.132), kind=kLoop, calls=%fused_computation.146 | loop fusion | flops 1048576 | bytes 8388608 | tf_op jit(solution)/shard_map/slice | solution.py:218
  57.7 5.9 %fusion.16 = f32[128,64,64]{2,1,0:T(8,128)} fusion(bf16[2,64,128,128,1,1,1]{3,1,6,5,2,0,4:T(8,128)(2,1)} %copy-done.1, bf16[128,1,32,128]{3,2,0,1:T(8,128)(2,1)} %get-tuple-element.14, bf16[128,1,32,128]{3,2,0,1:T(8,128)(2,1)S(1)} %get-tuple-element.13, bf16[128,2,32,128]{3,2,0,1:T(8,128)(2,1)S(1)} %bitcast.135), kind=kOutput, calls=%fused_computation.23 | convolution fusion | flops 281018368 | bytes 10485760 | tf_op jit(solution)/shard_map/rckm,rcum->rku/dot_general | solution.py:233
  63.6 5.0 %fusion.19 = f32[128,64,128]{2,1,0:T(8,128)S(1)} fusion(bf16[128,2,64,128]{3,2,1,0:T(8,128)(2,1)S(1)} %bitcast.133, bf16[128,1,64,128]{3,2,1,0:T(8,128)(2,1)} %get-tuple-element.10, bf16[128,1,64,128]{3,2,1,0:T(8,128)(2,1)} %get-tuple-element.9), kind=kOutput, calls=%fused_computation.24 | convolution fusion | flops 562036736 | bytes 12582912 | tf_op jit(solution)/shard_map/rckm,rclm->rkl/dot_general | solution.py:219
  68.7 1.1 slice_select_fusion
  69.8 1.0 copy-done.4
  70.8 3.1 %pad_maximum_fusion.1 = f32[128,64,128]{2,1,0:T(8,128)} fusion(f32[128,64,64]{2,1,0:T(8,128)S(1)} %copy-done.4, f32[128,64,64]{2,1,0:T(8,128)S(1)} %slice_select_fusion), kind=kLoop, calls=%fused_computation.18 | loop fusion | flops 1048576 | bytes 8388608 | tf_op jit(solution)/shard_map/concatenate | solution.py:234
  74.0 3.2 %dynamic-slice_bitcast_fusion = f32[2,2,2,8,64,128]{5,4,3,2,1,0:T(8,128)} fusion(f32[2,2,2,2,8,64,128]{6,5,4,3,2,1,0:T(8,128)} %bitcast.130, s32[]{:T(128)S(6)} %select_n.151), kind=kLoop, calls=%fused_computation.27 | loop fusion | bytes 4194308 | tf_op jit(solution)/shard_map/jit(dynamic_index_in_dim)/squeeze | solution.py:256
  77.2 0.4 collective-permute-start
  77.6 4.0 %collective-permute-done = f32[2,2,2,8,64,128]{5,4,3,2,1,0:T(8,128)S(1)} collective-permute-done((f32[2,2,2,8,64,128]{5,4,3,2,1,0:T(8,128)}, f32[2,2,2,8,64,128]{5,4,3,2,1,0:T(8,128)S(1)}, u32[]{:S(2)}, u32[]{:S(2)}) %collective-permute-start) | collective-permute-done | bytes 2097184 | tf_op jit(solution)/shard_map/ppermute | solution.py:258
  81.6 2.0 %bitcast_add_fusion = f32[2,2,2,8,64,128]{5,4,3,2,1,0:T(8,128)S(1)} fusion(f32[2,2,2,8,64,128]{5,4,3,2,1,0:T(8,128)S(1)} %collective-permute-done, f32[2,2,2,2,8,64,128]{6,5,4,3,2,1,0:T(8,128)} %bitcast.131, s32[]{:T(128)S(6)} %select_n.150), kind=kLoop, calls=%fused_computation.26 | loop fusion | flops 524288 | bytes 6291460 | tf_op jit(solution)/shard_map/add | solution.py:258
  83.6 0.0 copy-start.7
  83.6 0.0 copy-start.8
  83.6 0.2 fusion.73
  83.8 0.0 copy-start.5
  83.8 0.1 constant_dynamic-slice_fusion.3
  83.9 3.0 %collective-permute-start.1 = (f32[2,2,4,64,128]{4,3,2,0,1:T(8,128)S(1)}, f32[2,2,4,64,128]{4,3,2,0,1:T(8,128)S(1)}, u32[]{:S(2)}, u32[]{:S(2)}) collective-permute-start(f32[2,2,4,64,128]{4,3,2,0,1:T(8,128)S(1)} %bitcast.139), channel_id=1, source_target_pairs={{0,2},{1,3},{2,0},{3,1},{4,6},{5,7},{6,4},{7,5},{8,10},{9,11},{10,... | collective-permute-start | bytes 1572872 | tf_op jit(solution)/shard_map/ppermute | solution.py:258
  87.0 0.1 constant_dynamic-slice_fusion.1
  87.1 1.6 collective-permute-start.4
  88.7 10.4 %collective-permute-done.1 = f32[2,2,4,64,128]{4,3,2,0,1:T(8,128)S(1)} collective-permute-done((f32[2,2,4,64,128]{4,3,2,0,1:T(8,128)S(1)}, f32[2,2,4,64,128]{4,3,2,0,1:T(8,128)S(1)}, u32[]{:S(2)}, u32[]{:S(2)}) %collective-permute-start.1) | collective-permute-done | bytes 524320 | tf_op jit(solution)/shard_map/ppermute | solution.py:258
  99.2 0.1 bitcast_add_fusion.2
  99.3 1.8 %collective-permute-start.2 = (f32[2,4,64,128]{3,2,1,0:T(8,128)S(1)}, f32[2,4,64,128]{3,2,1,0:T(8,128)S(1)}, u32[]{:S(2)}, u32[]{:S(2)}) collective-permute-start(f32[2,4,64,128]{3,2,1,0:T(8,128)S(1)} %dynamic-slice_bitcast_fusion.2), channel_id=1, source_target_pairs={{0,4},{1,5},{2,6},{3,7},{4,0},{5,1},{6,2},{7,3},{8,12},{9,13},{10,... | collective-permute-start | bytes 786440 | tf_op jit(solution)/shard_map/ppermute | solution.py:258
  101.1 0.0 collective-permute-done.4
  101.1 0.1 bitcast_add_fusion.1
  101.2 1.6 collective-permute-start.5
  102.8 4.4 %collective-permute-done.2 = f32[2,4,64,128]{3,2,1,0:T(8,128)S(1)} collective-permute-done((f32[2,4,64,128]{3,2,1,0:T(8,128)S(1)}, f32[2,4,64,128]{3,2,1,0:T(8,128)S(1)}, u32[]{:S(2)}, u32[]{:S(2)}) %collective-permute-start.2) | collective-permute-done | bytes 262176 | tf_op jit(solution)/shard_map/ppermute | solution.py:258
  107.2 2.5 %collective-permute-start.3 = (f32[4,64,128]{2,1,0:T(8,128)S(1)}, f32[4,64,128]{2,1,0:T(8,128)S(1)}, u32[]{:S(2)}, u32[]{:S(2)}) collective-permute-start(f32[4,64,128]{2,1,0:T(8,128)S(1)} %dynamic-slice_bitcast_fusion.4), channel_id=1, source_target_pairs={{0,8},{1,9},{2,10},{3,11},{4,12},{5,13},{6,14},{7,15},{8,0},{9,1},... | collective-permute-start | bytes 393224 | tf_op jit(solution)/shard_map/ppermute | solution.py:258
  109.7 0.0 collective-permute-done.5
  109.8 1.4 collective-permute-start.6
  111.2 7.6 %collective-permute-done.3 = f32[4,64,128]{2,1,0:T(8,128)S(1)} collective-permute-done((f32[4,64,128]{2,1,0:T(8,128)S(1)}, f32[4,64,128]{2,1,0:T(8,128)S(1)}, u32[]{:S(2)}, u32[]{:S(2)}) %collective-permute-start.3) | collective-permute-done | bytes 131104 | tf_op jit(solution)/shard_map/ppermute | solution.py:258
  118.9 1.9 %collective-permute-done.6 = f32[4,64,128]{2,1,0:T(8,128)S(1)} collective-permute-done((f32[4,64,128]{2,1,0:T(8,128)S(1)}, f32[4,64,128]{2,1,0:T(8,128)S(1)}, u32[]{:S(2)}, u32[]{:S(2)}) %collective-permute-start.6) | collective-permute-done | bytes 131104 | tf_op jit(solution)/shard_map/ppermute | solution.py:258
  120.8 0.1 copy.89
  120.9 0.3 fusion.26
  121.2 0.9 pad_maximum_fusion.2.b_ref
  122.1 0.2 fusion.70
  122.2 1.0 maximum_maximum_fusion.1.a_ref
  123.2 22.1 %shard_map.55 = f32[8,128,32]{2,1,0:T(8,128)} custom-call(f32[8,128,128]{2,1,0:T(8,128)} %maximum_maximum_fusion.1.a_ref, f32[8,128,32]{2,1,0:T(8,128)} %pad_maximum_fusion.2.b_ref), custom_call_target="tpu_custom_call" | custom-call | tf_op jit(solution)/shard_map/pallas_call | solution.py:100
  145.3 1.2 copy.90
  146.5 0.2 reshape.335
  146.8 0.1 copy.92
  146.9 13.1 %all_to_all.18 = f32[64,1,2,256]{3,2,1,0:T(2,128)S(1)} all-to-all(f32[64,1,2,256]{3,2,1,0:T(2,128)S(1)} %copy.92), channel_id=1, replica_groups=mesh['cells'=2,'fh'=16] {'fh'}, dimensions={0} | all-to-all | bytes 262144 | tf_op jit(solution)/shard_map/all_to_all | solution.py:292
  160.0 0.7 copy.110
  (34 shorter events, 0.4 us)
Async XLA Ops:
  39.1 2.6 %copy-start = (bf16[3,2,16,256,128]{4,3,2,0,1:T(8,128)(2,1)}, bf16[3,2,16,256,128]{4,3,2,0,1:T(8,128)(2,1)S(1)}, u32[]{:S(2)}) copy-start(bf16[3,2,16,256,128]{4,3,2,0,1:T(8,128)(2,1)S(1)} %fusion.6) | copy-start | bytes 18874372
  42.0 2.7 %copy-start.6 = (s32[64]{0:T(128)S(1)}, s32[64]{0:T(128)}, u32[]{:S(2)}) copy-start(s32[64]{0:T(128)} %param.6) | copy-start | bytes 772
  42.0 2.9 %slice-start = ((bf16[3,2,16,256,128]{4,3,2,0,1:T(8,128)(2,1)}), bf16[2,2,16,256,128]{4,3,2,0,1:T(8,128)(2,1)S(1)}, s32[]{:S(2)}) async-start(bf16[3,2,16,256,128]{4,3,2,0,1:T(8,128)(2,1)} %copy-done), calls=%async_computation.1 | async-start | bytes 8388608 | tf_op jit(solution)/shard_map/slice | solution.py:286
  50.7 2.7 %copy-start.1 = (bf16[2,64,128,128,1,1,1]{3,1,6,5,2,0,4:T(8,128)(2,1)}, bf16[2,64,128,128,1,1,1]{3,1,6,5,2,0,4:T(8,128)(2,1)S(1)}, u32[]{:S(2)}) copy-start(bf16[2,64,128,128,1,1,1]{3,1,6,5,2,0,4:T(8,128)(2,1)S(1)} %fusion.10) | copy-start | bytes 12582916
  53.4 2.0 %copy-start.2 = (bf16[2,64,128,128,1,1,1]{3,1,0,2,4,5,6:T(8,128)(2,1)}, bf16[2,64,128,128,1,1,1]{3,1,0,2,4,5,6:T(8,128)(2,1)S(1)}, u32[]{:S(2)}) copy-start(bf16[2,64,128,128,1,1,1]{3,1,0,2,4,5,6:T(8,128)(2,1)S(1)} %copy.125) | copy-start | bytes 12582916
  57.7 5.9 %copy-start.3 = (bf16[2,64,128,128,1,1,1]{3,1,0,2,4,5,6:T(8,128)(2,1)S(1)}, bf16[2,64,128,128,1,1,1]{3,1,0,2,4,5,6:T(8,128)(2,1)}, u32[]{:S(2)}) copy-start(bf16[2,64,128,128,1,1,1]{3,1,0,2,4,5,6:T(8,128)(2,1)} %copy-done.2) | copy-start | bytes 12582916
  68.7 2.2 %copy-start.4 = (f32[128,64,64]{2,1,0:T(8,128)S(1)}, f32[128,64,64]{2,1,0:T(8,128)}, u32[]{:S(2)}) copy-start(f32[128,64,64]{2,1,0:T(8,128)} %fusion.16) | copy-start | bytes 6291460
  77.2 4.4 %collective-permute-start = (f32[2,2,2,8,64,128]{5,4,3,2,1,0:T(8,128)}, f32[2,2,2,8,64,128]{5,4,3,2,1,0:T(8,128)S(1)}, u32[]{:S(2)}, u32[]{:S(2)}) collective-permute-start(f32[2,2,2,8,64,128]{5,4,3,2,1,0:T(8,128)} %dynamic-slice_bitcast_fusion), channel_id=1, source_target_pairs={{0,1},{1,0},{2,3},{3,2},{4,5},{5,4},{6,7},{7,6},{8,9},{9,8},{10,11... | collective-permute-start | bytes 6291464 | tf_op jit(solution)/shard_map/ppermute | solution.py:258
  83.6 3.4 %copy-start.7 = (f32[64]{0:T(128)S(1)}, f32[64]{0:T(128)}, u32[]{:S(2)}) copy-start(f32[64]{0:T(128)} %param.9) | copy-start | bytes 772
  83.6 3.4 %copy-start.8 = (s32[64]{0:T(128)S(1)}, s32[64]{0:T(128)}, u32[]{:S(2)}) copy-start(s32[64]{0:T(128)} %param.7) | copy-start | bytes 772
  83.8 4.9 %copy-start.5 = (s32[8,64]{1,0:T(8,128)S(1)}, s32[8,64]{1,0:T(8,128)}, u32[]{:S(2)}) copy-start(s32[8,64]{1,0:T(8,128)} %param.8) | copy-start | bytes 6148
  83.9 15.2 %collective-permute-start.1 = (f32[2,2,4,64,128]{4,3,2,0,1:T(8,128)S(1)}, f32[2,2,4,64,128]{4,3,2,0,1:T(8,128)S(1)}, u32[]{:S(2)}, u32[]{:S(2)}) collective-permute-start(f32[2,2,4,64,128]{4,3,2,0,1:T(8,128)S(1)} %bitcast.139), channel_id=1, source_target_pairs={{0,2},{1,3},{2,0},{3,1},{4,6},{5,7},{6,4},{7,5},{8,10},{9,11},{10,... | collective-permute-start | bytes 1572872 | tf_op jit(solution)/shard_map/ppermute | solution.py:258
  87.1 14.0 %collective-permute-start.4 = (f32[2,2,4,64,128]{4,3,2,0,1:T(8,128)S(1)}, f32[2,2,4,64,128]{4,3,2,0,1:T(8,128)S(1)}, u32[]{:S(2)}, u32[]{:S(2)}) collective-permute-start(f32[2,2,4,64,128]{4,3,2,0,1:T(8,128)S(1)} %bitcast.140), channel_id=1, source_target_pairs={{0,4},{1,5},{2,6},{3,7},{4,0},{5,1},{6,2},{7,3},{8,12},{9,13},{10,... | collective-permute-start | bytes 1572872 | tf_op jit(solution)/shard_map/ppermute | solution.py:258
  99.3 7.9 %collective-permute-start.2 = (f32[2,4,64,128]{3,2,1,0:T(8,128)S(1)}, f32[2,4,64,128]{3,2,1,0:T(8,128)S(1)}, u32[]{:S(2)}, u32[]{:S(2)}) collective-permute-start(f32[2,4,64,128]{3,2,1,0:T(8,128)S(1)} %dynamic-slice_bitcast_fusion.2), channel_id=1, source_target_pairs={{0,4},{1,5},{2,6},{3,7},{4,0},{5,1},{6,2},{7,3},{8,12},{9,13},{10,... | collective-permute-start | bytes 786440 | tf_op jit(solution)/shard_map/ppermute | solution.py:258
  101.2 8.6 %collective-permute-start.5 = (f32[2,4,64,128]{3,2,1,0:T(8,128)S(1)}, f32[2,4,64,128]{3,2,1,0:T(8,128)S(1)}, u32[]{:S(2)}, u32[]{:S(2)}) collective-permute-start(f32[2,4,64,128]{3,2,1,0:T(8,128)S(1)} %dynamic-slice_bitcast_fusion.1), channel_id=1, source_target_pairs={{0,2},{1,3},{2,0},{3,1},{4,6},{5,7},{6,4},{7,5},{8,10},{9,11},{10,... | collective-permute-start | bytes 786440 | tf_op jit(solution)/shard_map/ppermute | solution.py:258
  107.2 11.6 %collective-permute-start.3 = (f32[4,64,128]{2,1,0:T(8,128)S(1)}, f32[4,64,128]{2,1,0:T(8,128)S(1)}, u32[]{:S(2)}, u32[]{:S(2)}) collective-permute-start(f32[4,64,128]{2,1,0:T(8,128)S(1)} %dynamic-slice_bitcast_fusion.4), channel_id=1, source_target_pairs={{0,8},{1,9},{2,10},{3,11},{4,12},{5,13},{6,14},{7,15},{8,0},{9,1},... | collective-permute-start | bytes 393224 | tf_op jit(solution)/shard_map/ppermute | solution.py:258
  109.8 10.9 %collective-permute-start.6 = (f32[4,64,128]{2,1,0:T(8,128)S(1)}, f32[4,64,128]{2,1,0:T(8,128)S(1)}, u32[]{:S(2)}, u32[]{:S(2)}) collective-permute-start(f32[4,64,128]{2,1,0:T(8,128)S(1)} %dynamic-slice_bitcast_fusion.3), channel_id=1, source_target_pairs={{0,8},{1,9},{2,10},{3,11},{4,12},{5,13},{6,14},{7,15},{8,0},{9,1},... | collective-permute-start | bytes 393224 | tf_op jit(solution)/shard_map/ppermute | solution.py:258
